TPU v7x, 512 devices: a whole 4x8x8 slice. The times are simulated.
512 devices in a mesh: nodes: 64 (over z, x, core), cams: 8 (over y).
Axes of the slice: x: 4, y: 8, z: 8, core: 2. Of those that a mesh axis runs over, the one named last changes fastest.
Arguments:
- iterate: float32 [1024, 12, 128], P(('nodes', 'cams')), may hold values from -6 to 6
- residual: float32 [1024, 12, 128], P(('nodes', 'cams')), may hold values from -6 to 6
- direction: float32 [1024, 12, 128], P(('nodes', 'cams')), may hold values from -5 to 5
- precond: float32 [1024, 12, 128], P(('nodes', 'cams')), may hold values from 0.2 to 6, as said below
- send_list: int32 [64, 64, 3], P('nodes'), may hold values from -1 to 15, as said below
- grads: bfloat16 [12, 1048576], P(None, ('nodes', 'cams')), may hold values from -2.390625 to 2.390625
- node_refs: int32 [4, 1048576], P(None, ('nodes', 'cams')), may hold values from 0 to 24575, as said below
- skin: bfloat16 [4, 1048576], P(None, ('nodes', 'cams')), may hold values from 0.099609375 to 1
- rigid_nbr: int32 [1024, 6, 128], P(('nodes', 'cams')), may hold values from 0 to 127, as said below
Outputs:
- new_iterate: float32 [1024, 12, 128], P(('nodes', 'cams'))
- new_residual: float32 [1024, 12, 128], P(('nodes', 'cams'))
- new_direction: float32 [1024, 12, 128], P(('nodes', 'cams'))
Inputs may be any that keep to these rules, and one draw needn't show every extreme that they name: `precond`: Positive. `send_list`: for each owner and receiver the live entries come first and the rest are -1; at most 3 live entries, and every receiver n has all 3 slots live from owner (n - 1) mod 64. `node_refs`: every reference names a live slot of its device's receiver; the 4 references of a pixel lie in the same slot. `rigid_nbr`: never the node itself.
All inputs are finite; a program needn't handle non-finite values.
Results may differ from a plain program's by a relative error of at most 0.00085.
Values sent between devices are 32-bit elements; how exact they have to be, the bound alone decides.
A program may use at most 64 MiB of HBM per device.

v0:
```python
import jax
import jax.numpy as jnp
from jax import lax
from jax.sharding import PartitionSpec as P

FRAMES = 8


temporal_weight = 0.5
rigid_weight = 0.1
highest = lax.Precision.HIGHEST


def shifted(value, axis, by):
    size = lax.axis_size(axis)
    pairs = [(i, i + by) for i in range(size) if 0 <= i + by < size]
    return lax.ppermute(value, axis, pairs)


def rigidity(patches, neighbours):
    node_width = patches.shape[2]
    columns = jnp.arange(node_width, dtype=jnp.int32)
    end_hits = (neighbours[..., None] == columns).astype(jnp.float32)
    identity = (columns[:, None] == columns[None, :]).astype(jnp.float32)
    edge_rows = identity[None, None] - end_hits
    laplace = jnp.einsum("qrim,qrin->qmn", edge_rows, edge_rows, precision=highest)
    return rigid_weight * jnp.einsum("qfm,qmn->qfn", patches, laplace, precision=highest)


def on_device(iterate, residual, direction, precond, send_list, grads, node_refs, skin, rigid_nbr):
    params = direction.shape[1]
    node_width = direction.shape[2]
    owned = lax.all_gather(direction, "cams", axis=0, tiled=True)
    held_count = owned.shape[0]
    peer_count = send_list.shape[1]
    slot_count = send_list.shape[2]
    chosen = (
        send_list[0].reshape(-1)[:, None] == jnp.arange(held_count, dtype=jnp.int32)[None, :]
    ).astype(jnp.float32)
    outgoing = jnp.einsum("sq,qfn->fsn", chosen, owned, precision=highest)
    outgoing = outgoing.reshape(params, peer_count, slot_count, node_width)
    incoming = lax.all_to_all(outgoing, "nodes", split_axis=1, concat_axis=1, tiled=True)
    visible = incoming.reshape(params, -1)
    grad_values = grads.astype(jnp.float32)
    weights = skin.astype(jnp.float32)
    values = visible[:, node_refs]
    projected = jnp.sum(values * grad_values[:, None, :], axis=0)
    response = jnp.sum(weights * projected, axis=0)
    scattered = (weights * response[None])[None] * grad_values[:, None, :]
    returns_local = jnp.zeros_like(visible).at[:, node_refs].add(scattered)
    returns_local = returns_local.reshape(params, peer_count, slot_count, node_width)
    arrived = lax.all_to_all(returns_local, "nodes", split_axis=1, concat_axis=1, tiled=True)
    summed = jnp.einsum(
        "sq,fsn->qfn",
        chosen,
        arrived.reshape(params, peer_count * slot_count, node_width),
        precision=highest,
    )
    data_image = lax.psum_scatter(summed, "cams", scatter_dimension=0, tiled=True)
    device_step = lax.axis_size(("nodes", "cams")) // FRAMES
    earlier = shifted(direction, ("nodes", "cams"), device_step)
    following = shifted(direction, ("nodes", "cams"), -device_step)
    temporal_part = temporal_weight * (2.0 * direction - earlier - following)
    image_all = data_image + rigidity(direction, rigid_nbr) + temporal_part
    scaled = precond * residual
    start_norm = lax.psum(jnp.sum(residual * scaled), ("nodes", "cams"))
    curvature = lax.psum(jnp.sum(direction * image_all), ("nodes", "cams"))
    step_length = start_norm / curvature
    new_residual = residual - step_length * image_all
    scaled_new = precond * new_residual
    new_norm = lax.psum(jnp.sum(new_residual * scaled_new), ("nodes", "cams"))
    new_iterate = iterate + step_length * direction
    new_direction = scaled_new + new_norm / start_norm * direction
    return (new_iterate, new_residual, new_direction)


def solution(mesh):
    in_specs = (
        P(("nodes", "cams"), None, None),
        P(("nodes", "cams"), None, None),
        P(("nodes", "cams"), None, None),
        P(("nodes", "cams"), None, None),
        P("nodes", None, None),
        P(None, ("nodes", "cams")),
        P(None, ("nodes", "cams")),
        P(None, ("nodes", "cams")),
        P(("nodes", "cams"), None, None),
    )
    out_specs = (
        P(("nodes", "cams"), None, None),
        P(("nodes", "cams"), None, None),
        P(("nodes", "cams"), None, None),
    )
    return jax.shard_map(
        on_device, mesh=mesh, in_specs=in_specs, out_specs=out_specs, check_vma=False
    )
```

profile of v0, /device:TPU:1, one launch (start us, length us, event | category | flops | bytes accessed | tf_op | source)
XLA Modules:
  0.0 522.1 jit_solution(3805391587379272148)
XLA Ops:
  7.2 0.7 copy.40
  7.9 20.6 %all_gather.3 = f32[16,12,128]{2,1,0:T(8,128)S(1)} all-gather(f32[2,12,128]{2,1,0:T(8,128)S(1)} %copy.40), channel_id=1, replica_groups=mesh['nodes'=64,'cams'=8] {'cams'}, dimensions={0}, use_global_device_ids=true | all-gather | bytes 110592 | tf_op jit(solution)/shard_map/all_gather | solution.py:33
  28.5 0.8 copy.25
  29.4 0.7 convolution_bitcast_fusion
  30.1 0.5 reshape.36
  30.6 1.4 copy.28
  32.1 20.4 %all-to-all-start = ((f32[12,64,3,128]{3,2,0,1:T(4,128)}), f32[12,64,3,128]{3,2,0,1:T(4,128)S(1)}, u32[]{:S(2)}, u32[]{:S(2)}) async-start(f32[12,64,3,128]{3,2,0,1:T(4,128)} %copy.28), calls=%async_computation | async-start | bytes 3145728 | tf_op jit(solution)/shard_map/all_to_all | solution.py:42
  52.8 38.7 %all-to-all-done = f32[12,64,3,128]{3,2,0,1:T(4,128)S(1)} async-done(((f32[12,64,3,128]{3,2,0,1:T(4,128)}), f32[12,64,3,128]{3,2,0,1:T(4,128)S(1)}, u32[]{:S(2)}, u32[]{:S(2)}) %all-to-all-start) | async-done | bytes 1179680 | tf_op jit(solution)/shard_map/all_to_all | solution.py:42
  91.5 7.1 %copy.29 = f32[12,64,3,128]{0,3,2,1:T(8,128)} copy(f32[12,64,3,128]{3,2,0,1:T(4,128)S(1)} %all-to-all-done) | data formatting | bytes 2359296 | tf_op jit(solution)/shard_map/all_to_all | solution.py:42
  98.6 32.3 %gather_fusion = f32[8192,12]{1,0:T(8,128)} fusion(f32[12,24576]{0,1:T(8,128)} %bitcast.30, s32[8192]{0:T(1024)S(1)} %broadcast_clamp_fusion), kind=kCustom, calls=%fused_computation | custom fusion | bytes 819200 | tf_op jit(solution)/shard_map/gather | solution.py:46
  130.9 3.3 multiply_reduce_fusion
  134.3 3.1 broadcast_multiply_fusion
  137.3 49.6 %scatter_custom_fusion = f32[12,24576]{0,1:T(8,128)} fusion(s32[8192]{0:T(1024)S(1)} %bitcast.34, f32[8192,12]{1,0:T(8,128)} %bitcast.32, f32[]{:T(128)} %constant.6.clone.1), kind=kCustom, calls=%fused_computation.2 | custom fusion | flops 98304 | bytes 1180160 | tf_op jit(solution)/shard_map/scatter-add | solution.py:50
  187.0 9.3 %copy.31 = f32[12,64,3,128]{3,2,0,1:T(4,128)} copy(f32[12,64,3,128]{0,3,2,1:T(8,128)} %bitcast.29) | data formatting | bytes 2359296 | tf_op jit(solution)/shard_map/reshape | solution.py:51
  196.3 6.4 %all-to-all-start.1 = ((f32[12,64,3,128]{3,2,0,1:T(4,128)}), f32[12,64,3,128]{3,2,0,1:T(4,128)S(1)}, u32[]{:S(2)}, u32[]{:S(2)}) async-start(f32[12,64,3,128]{3,2,0,1:T(4,128)} %copy.31), calls=%async_computation.1 | async-start | bytes 3145728 | tf_op jit(solution)/shard_map/all_to_all | solution.py:52
  202.8 3.3 collective-permute-start
  206.0 1.5 collective-permute-start.1
  207.5 1.3 dynamic-slice
  209.5 1.0 convolution_bitcast_fusion.1
  210.5 31.5 %all-to-all-done.1 = f32[12,64,3,128]{3,2,0,1:T(4,128)S(1)} async-done(((f32[12,64,3,128]{3,2,0,1:T(4,128)}), f32[12,64,3,128]{3,2,0,1:T(4,128)S(1)}, u32[]{:S(2)}, u32[]{:S(2)}) %all-to-all-start.1) | async-done | bytes 1179680 | tf_op jit(solution)/shard_map/all_to_all | solution.py:52
  242.4 0.6 reshape.39
  243.0 1.1 fusion.16
  244.2 0.6 fusion.19
  244.8 67.6 %all-reduce.4.cloned.1.call-done = f32[16,12,128]{2,0,1:T(8,128)} async-done(((f32[16,12,128]{2,0,1:T(8,128)}), f32[16,12,128]{2,0,1:T(8,128)}) %all-reduce.4.cloned.1.call-update) | async-done | bytes 98320
  312.5 0.8 constant_dynamic-slice_fusion
  313.3 0.8 multiply_reduce_fusion.1
  314.1 102.7 %all-reduce.1 = (f32[]{:T(128)}, f32[]{:T(128)}) all-reduce(f32[]{:T(128)} %fusion.19, f32[]{:T(128)} %get-tuple-element.12), channel_id=1, replica_groups=mesh['nodes'=64,'cams'=8] {'nodes','cams'}, use_global_device_ids=true, to_apply=%region_1.0 | all-reduce | flops 2 | bytes 16 | tf_op jit(solution)/shard_map/psum | solution.py:66
  418.1 0.6 fusion.14
  418.7 93.3 %psum.23 = f32[]{:T(128)} all-reduce(f32[]{:T(128)} %get-tuple-element.8), channel_id=1, replica_groups=mesh['nodes'=64,'cams'=8] {'nodes','cams'}, use_global_device_ids=true, to_apply=%region_9.0 | all-reduce | flops 1 | bytes 8 | tf_op jit(solution)/shard_map/psum | solution.py:71
  513.4 0.6 copy.47
  514.1 0.6 copy.46
  514.7 0.6 copy.48
  (31 shorter events, 0.9 us)
Async XLA Ops:
  30.1 22.4 %copy-start.5 = (s32[4,2048]{1,0:T(4,128)S(1)}, s32[4,2048]{1,0:T(4,128)}, u32[]{:S(2)}) copy-start(s32[4,2048]{1,0:T(4,128)} %param.15) | copy-start | bytes 98308
  30.1 22.4 %copy-start.2 = (bf16[12,2048]{1,0:T(8,128)(2,1)S(1)}, bf16[12,2048]{1,0:T(8,128)(2,1)}, u32[]{:S(2)}) copy-start(bf16[12,2048]{1,0:T(8,128)(2,1)} %param.14) | copy-start | bytes 147460
  32.1 59.4 %all-to-all-start = ((f32[12,64,3,128]{3,2,0,1:T(4,128)}), f32[12,64,3,128]{3,2,0,1:T(4,128)S(1)}, u32[]{:S(2)}, u32[]{:S(2)}) async-start(f32[12,64,3,128]{3,2,0,1:T(4,128)} %copy.28), calls=%async_computation | async-start | bytes 3145728 | tf_op jit(solution)/shard_map/all_to_all | solution.py:42
  98.6 35.6 %copy-start.3 = (bf16[4,2048]{1,0:T(4,128)(2,1)S(1)}, bf16[4,2048]{1,0:T(4,128)(2,1)}, u32[]{:S(2)}) copy-start(bf16[4,2048]{1,0:T(4,128)(2,1)} %param.16) | copy-start | bytes 49156
  187.0 20.5 %copy-start.7 = (s32[2,6,128]{2,0,1:T(2,128)S(1)}, s32[2,6,128]{2,0,1:T(2,128)}, u32[]{:S(2)}) copy-start(s32[2,6,128]{2,0,1:T(2,128)} %param.17) | copy-start | bytes 18436
  196.3 45.8 %all-to-all-start.1 = ((f32[12,64,3,128]{3,2,0,1:T(4,128)}), f32[12,64,3,128]{3,2,0,1:T(4,128)S(1)}, u32[]{:S(2)}, u32[]{:S(2)}) async-start(f32[12,64,3,128]{3,2,0,1:T(4,128)} %copy.31), calls=%async_computation.1 | async-start | bytes 3145728 | tf_op jit(solution)/shard_map/all_to_all | solution.py:52
  202.7 41.5 %copy-start.1 = (f32[2,12,128]{2,0,1:T(2,128)S(1)}, f32[2,12,128]{2,0,1:T(2,128)}, u32[]{:S(2)}) copy-start(f32[2,12,128]{2,0,1:T(2,128)} %param.12) | copy-start | bytes 36868
  202.7 41.5 %copy-start.4 = (f32[2,12,128]{2,0,1:T(2,128)S(1)}, f32[2,12,128]{2,0,1:T(2,128)}, u32[]{:S(2)}) copy-start(f32[2,12,128]{2,0,1:T(2,128)} %param.10) | copy-start | bytes 36868
  202.7 110.6 %copy-start = (f32[2,12,128]{2,0,1:T(2,128)S(1)}, f32[2,12,128]{2,0,1:T(2,128)}, u32[]{:S(2)}) copy-start(f32[2,12,128]{2,0,1:T(2,128)} %param.11) | copy-start | bytes 36868
  202.7 109.8 %all-reduce.4.cloned.1.call-start = ((), (), s32[]{:S(2)}) async-start(), calls=%async_computation.2 | async-start | bytes 196608
  202.8 110.5 %collective-permute-start = (f32[2,12,128]{2,1,0:T(8,128)S(1)}, f32[2,12,128]{2,1,0:T(8,128)S(1)}, u32[]{:S(2)}, u32[]{:S(2)}) collective-permute-start(f32[2,12,128]{2,1,0:T(8,128)S(1)} %copy.40), channel_id=1, source_target_pairs={{0,64},{1,65},{2,66},{3,67},{4,68},{5,69},{6,70},{7,71},{8,72},{9,... | collective-permute-start | bytes 36872 | tf_op jit(solution)/shard_map/ppermute | solution.py:17
  206.0 107.3 %collective-permute-start.1 = (f32[2,12,128]{2,1,0:T(8,128)S(1)}, f32[2,12,128]{2,1,0:T(8,128)S(1)}, u32[]{:S(2)}, u32[]{:S(2)}) collective-permute-start(f32[2,12,128]{2,1,0:T(8,128)S(1)} %copy.40), channel_id=1, source_target_pairs={{64,0},{65,1},{66,2},{67,3},{68,4},{69,5},{70,6},{71,7},{72,8},{73... | collective-permute-start | bytes 36872 | tf_op jit(solution)/shard_map/ppermute | solution.py:17
  209.5 304.6 %copy-start.6 = (f32[2,12,128]{2,0,1:T(2,128)S(1)}, f32[2,12,128]{2,0,1:T(2,128)}, u32[]{:S(2)}) copy-start(f32[2,12,128]{2,0,1:T(2,128)} %param.9) | copy-start | bytes 36868
Sparse Core Ops, SparseCore 0:
  244.3 68.0 all-reduce.3
where the time goes:
time: 523 us; the launch traced here: 522 us
  blocking collectives  217 us (41%)
  waiting for transfers between devices  138 us (26%)
  local copies, waits for them, and re-layouts  57.4 us (11%)
  other arithmetic  57.4 us (11%)
  starting transfers between devices  31.5 us (6%)
  between operations  17.6 us (3%)
    psum x1, blocking collectives, on_device(): start_norm = lax.psum(jnp.sum(residual * scaled), ('nodes', 'cams'))  103 us
    psum x1, blocking collectives, on_device(): new_norm = lax.psum(jnp.sum(new_residual * scaled_new), ('nodes', 'cams'))  93.3 us
    unnamed x2, waiting for transfers between devices  67.6 us
    scatter-add x1, other arithmetic, on_device(): returns_local = jnp.zeros_like(visible).at[:, node_refs].add(scattered)  49.6 us
    all_to_all x1, waiting for transfers between devices, on_device(): lax.all_to_all(outgoing, 'nodes', split_axis=1, concat_axis=1, tiled=True)  38.7 us
    gather x1, local copies, waits for them, and re-layouts, on_device(): values = visible[:, node_refs]  32.3 us
    all_to_all x1, waiting for transfers between devices, on_device(): lax.all_to_all(returns_local, 'nodes', split_axis=1, concat_axis=1, tiled...  31.5 us
    all_gather x1, blocking collectives, on_device(): owned = lax.all_gather(direction, 'cams', axis=0, tiled=True)  20.6 us
  transfers between devices with their start and end apart: 5, of which 3 were waited for; matrix products, arithmetic and copies ran while one was open for 1% of the time, Pallas kernels for 0%

commit v1 on v0

v1 whole, which is shorter than its diff:
```python
import functools

import jax
import jax.numpy as jnp
from jax import lax
from jax.experimental import pallas as pl
from jax.experimental.pallas import tpu as pltpu
from jax.sharding import PartitionSpec as P

MESH = pl.DeviceIdType.MESH
FRAMES = 8
HALVES = 2
temporal_weight = 0.5
rigid_weight = 0.1

OWNED, PIXELS, GRADS, RESID, PREC, SMOOTH, PARTIAL, TOTAL, IMAGE, SUMS = range(10)
VISIBLE, RETURNS, NODE_SUMS = range(3)


def split(value):
    high = value.astype(jnp.bfloat16)
    return high, (value - high.astype(jnp.float32)).astype(jnp.bfloat16)


def dot(left, right, contract):
    return lax.dot_general(left, right, (contract, ((), ())), preferred_element_type=jnp.float32)


def kernel(
    node_count, cam_count, tile,
    iterate, residual, direction, precond, send_list, grads, node_refs, skin, rigid_nbr,
    new_iterate, new_residual, new_direction,
    pixels, grad_send, grad_rows, one_hot, weight,
    owned_recv, resid_recv, prec_recv, smooth_send, smooth_recv, frame_recv,
    owned, owned_resid, owned_prec, owned_smooth,
    chosen, visible_send, visible_recv, table, partial, partial_recv, total, returned, square,
    returns_send, returns_recv, image_send, image_recv, image,
    node_sums, cam_sums, cam_send,
    cam_send_sem, cam_recv_sem, node_send_sem, node_recv_sem, frame_send_sem, frame_recv_sem,
):
    me_node = lax.axis_index("nodes")
    me_cam = lax.axis_index("cams")
    group = me_cam // HALVES
    half = lax.rem(me_cam, HALVES)
    params, local, width = direction.shape
    slots = send_list.shape[0]
    per_group = grad_send.shape[1]
    span = width // HALVES
    rows = per_group * span
    keys = slots * node_count
    pixel_count = node_refs.shape[1]
    held = local * cam_count
    first = group * per_group
    frame_step = node_count // FRAMES

    barrier = pltpu.get_barrier_semaphore()

    def greet_cam(k, carry):
        pl.semaphore_signal(barrier, inc=1, device_id={"cams": lax.rem(me_cam + k, cam_count)}, device_id_type=MESH)
        return carry

    def greet_node(k, carry):
        pl.semaphore_signal(barrier, inc=1, device_id={"nodes": lax.rem(me_node + k, node_count)}, device_id_type=MESH)
        return carry

    lax.fori_loop(1, cam_count, greet_cam, 0)
    lax.fori_loop(1, node_count, greet_node, 0)

    def to_cam(phase, source, target, k):
        slot = lax.rem(cam_count - k, cam_count)
        return pltpu.make_async_remote_copy(
            src_ref=source, dst_ref=target.at[slot],
            send_sem=cam_send_sem.at[phase, k], recv_sem=cam_recv_sem.at[phase, slot],
            device_id={"cams": lax.rem(me_cam + k, cam_count)}, device_id_type=MESH,
        )

    def from_cam(phase, target, k):
        return pltpu.make_async_remote_copy(
            src_ref=target.at[k], dst_ref=target.at[k],
            send_sem=cam_send_sem.at[phase, k], recv_sem=cam_recv_sem.at[phase, k],
            device_id={"cams": lax.rem(me_cam + k, cam_count)}, device_id_type=MESH,
        )

    def to_node(phase, source, target, k, indexed):
        peer = lax.rem(me_node + k, node_count)
        return pltpu.make_async_remote_copy(
            src_ref=source.at[peer] if indexed else source.at[me_node], dst_ref=target.at[me_node],
            send_sem=node_send_sem.at[phase, k], recv_sem=node_recv_sem.at[phase, me_node],
            device_id={"nodes": peer}, device_id_type=MESH,
        )

    def from_node(phase, target, k):
        peer = lax.rem(me_node + k, node_count)
        return pltpu.make_async_remote_copy(
            src_ref=target.at[peer], dst_ref=target.at[peer],
            send_sem=node_send_sem.at[phase, k], recv_sem=node_recv_sem.at[phase, peer],
            device_id={"nodes": peer}, device_id_type=MESH,
        )

    def send_nodes(phase, source, target, indexed=True):
        def one(k, carry):
            to_node(phase, source, target, k, indexed).start()
            return carry
        lax.fori_loop(1, node_count, one, 0)

    def wait_nodes(phase, target):
        def one(k, carry):
            from_node(phase, target, k).wait_recv()
            return carry
        lax.fori_loop(1, node_count, one, 0)

    def near(i):
        return jnp.where(lax.rem(i, 2) == 1, (i + 1) // 2, lax.rem(cam_count - i // 2, cam_count))

    def each_cam(body, reverse=False, start=1):
        def one(i, carry):
            body(near(cam_count - 1 - i if reverse else i))
            return carry
        if reverse:
            lax.fori_loop(0, cam_count - start, one, 0)
        else:
            lax.fori_loop(start, cam_count, one, 0)

    pixels[0, 0:4, :] = node_refs[...].astype(jnp.float32)
    pixels[0, 4:8, :] = skin[...].astype(jnp.float32)
    grad_all = grads[...].astype(jnp.float32)
    for g in range(params // per_group):
        grad_send[g] = grad_all[g * per_group:(g + 1) * per_group]
    grad_rows[0] = grad_send[group]
    visible_send[...] = jnp.zeros_like(visible_send)
    returns_send[...] = jnp.zeros_like(returns_send)
    owned_recv[0] = direction[pl.ds(first, per_group)]
    resid_recv[0] = residual[pl.ds(first, per_group)]
    prec_recv[0] = precond[pl.ds(first, per_group)]

    pl.semaphore_wait(barrier, cam_count - 1 + node_count - 1)

    def peer_group(k):
        return lax.rem(me_cam + k, cam_count) // HALVES

    def peer_params(source, k):
        return source.at[pl.ds(peer_group(k) * per_group, per_group)]

    each_cam(lambda k: to_cam(OWNED, peer_params(direction, k), owned_recv, k).start())

    def to_frame(which):
        by = frame_step if which == 0 else node_count - frame_step
        return pltpu.make_async_remote_copy(
            src_ref=direction, dst_ref=frame_recv.at[which],
            send_sem=frame_send_sem.at[which], recv_sem=frame_recv_sem.at[which],
            device_id={"nodes": lax.rem(me_node + by, node_count)}, device_id_type=MESH,
        )

    to_frame(0).start()
    to_frame(1).start()

    def send_pixels(k):
        to_cam(PIXELS, pixels.at[0], pixels, k).start()
        to_cam(GRADS, grad_send.at[peer_group(k)], grad_rows, k).start()

    each_cam(send_pixels)

    def build(k):
        def one(i, carry):
            at = pl.ds(pl.multiple_of(i * tile, tile), tile)
            block = pixels[k, :, at]
            refs = block[0:4].astype(jnp.int32)
            weights = block[4:8]
            place = refs[0:1] >> 7
            source = (place * 171) >> 9
            key = (place - slots * source) * node_count + source
            hits = lax.broadcasted_iota(jnp.int32, (keys, tile), 0) == key
            one_hot[k, :, at] = jnp.where(hits, 1.0, 0.0).astype(jnp.bfloat16)
            within = (refs & (width - 1)) - half * span
            ids = lax.broadcasted_iota(jnp.int32, (span, tile), 0)
            summed = jnp.zeros((span, tile), jnp.float32)
            for s in range(4):
                summed = summed + jnp.where(ids == within[s:s + 1], weights[s:s + 1], 0.0)
            weight[k, :, at] = summed
            return carry
        lax.fori_loop(0, pixel_count // tile, one, 0)

    build(0)

    wanted = lax.broadcasted_iota(jnp.int32, (held, node_count), 0)
    for j in range(slots):
        listed = send_list[j]
        shifted = lax.rem(listed // local + cam_count - me_cam, cam_count) * local + lax.rem(listed, local)
        shifted = jnp.where(listed >= 0, shifted, -1)
        chosen[:, j * node_count:(j + 1) * node_count] = jnp.where(wanted == shifted, 1.0, 0.0)

    def take_half(value):
        return jnp.where(half == 0, value[:, :span], value[:, span:])

    def gather_owned(received, target):
        for k in range(cam_count):
            for f in range(per_group):
                target[f, k * local:(k + 1) * local, :] = received[k, f]

    def halves(target):
        return jnp.concatenate([take_half(target[f]) for f in range(per_group)], axis=1)

    each_cam(lambda k: from_cam(OWNED, owned_recv, k).wait_recv())
    gather_owned(owned_recv, owned)
    mine = halves(owned)
    one_hot_rows = chosen[...].astype(jnp.bfloat16)
    high, low = split(mine)
    listed_rows = dot(one_hot_rows, high, ((0,), (0,))) + dot(one_hot_rows, low, ((0,), (0,)))
    for j in range(slots):
        visible_send[:, j, 0:rows] = listed_rows[j * node_count:(j + 1) * node_count]
    visible_recv[pl.ds(me_node, 1)] = visible_send[pl.ds(me_node, 1)]
    send_nodes(VISIBLE, visible_send, visible_recv)

    each_cam(lambda k: to_cam(RESID, peer_params(residual, k), resid_recv, k).start())
    each_cam(lambda k: to_cam(PREC, peer_params(precond, k), prec_recv, k).start())
    to_frame(0).wait_recv()
    to_frame(1).wait_recv()
    ids = lax.broadcasted_iota(jnp.int32, (width, width), 0)
    lanes = lax.broadcasted_iota(jnp.int32, (width, width), 1)
    identity = jnp.where(ids == lanes, 1.0, 0.0)
    has_earlier = jnp.where(me_node >= frame_step, 1.0, 0.0)
    has_following = jnp.where(me_node < node_count - frame_step, 1.0, 0.0)
    for q in range(local):
        edges = jnp.concatenate(
            [identity - jnp.where(ids == rigid_nbr[r, q:q + 1, :], 1.0, 0.0) for r in range(rigid_nbr.shape[0])], axis=1
        ).astype(jnp.bfloat16)
        patch = jnp.concatenate([direction[f, q:q + 1, :] for f in range(params)], axis=0)
        high, low = split(patch)
        difference = dot(high, edges, ((1,), (0,))) + dot(low, edges, ((1,), (0,)))
        high, low = split(difference)
        rigid = dot(high, edges, ((1,), (1,))) + dot(low, edges, ((1,), (1,)))
        for f in range(params):
            here = direction[f, q:q + 1, :]
            time = 2.0 * here - has_earlier * frame_recv[0, f, q:q + 1, :] - has_following * frame_recv[1, f, q:q + 1, :]
            smooth_send[f, q:q + 1, :] = rigid_weight * rigid[f:f + 1] + temporal_weight * time
    smooth_recv[0] = smooth_send[pl.ds(first, per_group)]
    each_cam(lambda k: to_cam(SMOOTH, peer_params(smooth_send, k), smooth_recv, k).start())

    def build_peer(k):
        from_cam(PIXELS, pixels, k).wait_recv()
        build(k)

    each_cam(build_peer)

    wait_nodes(VISIBLE, visible_recv)
    for j in range(slots):
        high, low = split(visible_recv[:, j, 0:rows])
        table[j * node_count:(j + 1) * node_count, 0:rows] = high
        table[j * node_count:(j + 1) * node_count, rows:2 * rows] = low

    def project(k):
        @pl.when(k != 0)
        def _():
            from_cam(GRADS, grad_rows, k).wait_recv()

        def one(i, carry):
            at = pl.ds(pl.multiple_of(i * tile, tile), tile)
            picked = dot(table[...], one_hot[k, :, at], ((0,), (0,)))
            g = grad_rows[k, :, at]
            summed = jnp.zeros((span, tile), jnp.float32)
            for f in range(per_group):
                piece = picked[f * span:(f + 1) * span] + picked[rows + f * span:rows + (f + 1) * span]
                summed = summed + piece * g[f:f + 1]
            partial[k, :, at] = jnp.sum(summed * weight[k, :, at], axis=0, keepdims=True)
            return carry
        lax.fori_loop(0, pixel_count // tile, one, 0)

        @pl.when(k != 0)
        def _():
            to_cam(PARTIAL, partial.at[k], partial_recv, k).start()

    each_cam(project, reverse=True, start=0)

    partial_recv[0] = partial[0]
    each_cam(lambda k: from_cam(PARTIAL, partial_recv, k).wait_recv())
    summed = partial_recv[0]
    for k in range(1, cam_count):
        summed = summed + partial_recv[k]
    total[0] = summed
    each_cam(lambda k: to_cam(TOTAL, total.at[0], total, k).start(), reverse=True)

    returned[...] = jnp.zeros_like(returned)

    def give_back(k):
        @pl.when(k != 0)
        def _():
            from_cam(TOTAL, total, k).wait_recv()

        def one(i, carry):
            at = pl.ds(pl.multiple_of(i * tile, tile), tile)
            scaled = grad_rows[k, :, at] * total[k, :, at]
            w = weight[k, :, at]
            products = jnp.concatenate([w * scaled[f:f + 1] for f in range(per_group)], axis=0)
            high, low = split(products)
            both = jnp.concatenate([high, low], axis=0)
            returned[...] += dot(both, one_hot[k, :, at], ((1,), (1,)))
            return carry
        lax.fori_loop(0, pixel_count // tile, one, 0)

    each_cam(give_back, start=0)
    square[...] = jnp.zeros_like(square)
    square[0:rows, 0:keys] = returned[0:rows] + returned[rows:2 * rows]
    by_key = jnp.transpose(square[...])
    for j in range(slots):
        returns_send[:, j, 0:rows] = by_key[j * node_count:(j + 1) * node_count, 0:rows]
    returns_recv[pl.ds(me_node, 1)] = returns_send[pl.ds(me_node, 1)]
    send_nodes(RETURNS, returns_send, returns_recv)

    start_norm = jnp.sum(residual[...] * precond[...] * residual[...], axis=(0, 1))[None]
    each_cam(lambda k: from_cam(RESID, resid_recv, k).wait_recv())
    each_cam(lambda k: from_cam(PREC, prec_recv, k).wait_recv())
    each_cam(lambda k: from_cam(SMOOTH, smooth_recv, k).wait_recv())
    gather_owned(resid_recv, owned_resid)
    gather_owned(prec_recv, owned_prec)
    gather_owned(smooth_recv, owned_smooth)
    mine = halves(owned)
    mine_prec = halves(owned_prec)
    weighted_resid = halves(owned_resid) * mine_prec

    wait_nodes(RETURNS, returns_recv)
    pieces = halves(owned_smooth)
    one_hot_rows = chosen[...].astype(jnp.bfloat16)
    for j in range(slots):
        high, low = split(returns_recv[:, j, 0:rows])
        part = one_hot_rows[:, j * node_count:(j + 1) * node_count]
        pieces = pieces + dot(part, high, ((1,), (0,))) + dot(part, low, ((1,), (0,)))

    lane = lax.broadcasted_iota(jnp.int32, (1, width), 1)

    def spread(value, which):
        return jnp.where(lane == which, jnp.sum(value), 0.0)

    mine_sums = (
        spread(start_norm, 0) + spread(mine * pieces, 1) + spread(weighted_resid * pieces, 2)
        + spread(mine_prec * pieces * pieces, 3)
    )
    node_sums[pl.ds(me_node, 1)] = mine_sums[None]
    send_nodes(NODE_SUMS, node_sums, node_sums, indexed=False)

    for f in range(per_group):
        piece = pieces[:, f * span:(f + 1) * span]
        doubled = jnp.concatenate([piece, piece], axis=1)
        for k in range(cam_count):
            image_send[k, f] = doubled[k * local:(k + 1) * local]
    image_recv[0] = image_send[0]
    each_cam(lambda k: to_cam(IMAGE, image_send.at[k], image_recv, k).start())

    wait_nodes(NODE_SUMS, node_sums)
    cam_send[0] = jnp.sum(node_sums[...], axis=0)
    cam_sums[0] = cam_send[0]
    each_cam(lambda k: to_cam(SUMS, cam_send.at[0], cam_sums, k).start())

    each_cam(lambda k: from_cam(IMAGE, image_recv, k).wait_recv())
    lane2 = lax.broadcasted_iota(jnp.int32, (local, width), 1)
    for g in range(params // per_group):
        for f in range(per_group):
            sides = [
                image_recv[lax.rem(HALVES * g + s + cam_count - me_cam, cam_count), f] for s in range(HALVES)
            ]
            image[g * per_group + f] = jnp.where(lane2 < span, sides[0], sides[1])

    each_cam(lambda k: from_cam(SUMS, cam_sums, k).wait_recv())
    sums = jnp.sum(cam_sums[...], axis=0)

    def value_of(which):
        return jnp.sum(jnp.where(lane == which, sums, 0.0), axis=1, keepdims=True)

    start, curvature, cross, square_norm = (value_of(which) for which in range(4))
    step = start / curvature
    new_norm = start - 2.0 * step * cross + step * step * square_norm
    ratio = new_norm / start
    for f in range(params):
        new_iterate[f] = iterate[f] + step * direction[f]
        left = residual[f] - step * image[f]
        new_residual[f] = left
        new_direction[f] = precond[f] * left + ratio * direction[f]

    def sent(k):
        to_cam(OWNED, peer_params(direction, k), owned_recv, k).wait_send()
        to_cam(PIXELS, pixels.at[0], pixels, k).wait_send()
        to_cam(GRADS, grad_send.at[peer_group(k)], grad_rows, k).wait_send()
        to_cam(RESID, peer_params(residual, k), resid_recv, k).wait_send()
        to_cam(PREC, peer_params(precond, k), prec_recv, k).wait_send()
        to_cam(SMOOTH, peer_params(smooth_send, k), smooth_recv, k).wait_send()
        to_cam(PARTIAL, partial.at[k], partial_recv, k).wait_send()
        to_cam(TOTAL, total.at[0], total, k).wait_send()
        to_cam(IMAGE, image_send.at[k], image_recv, k).wait_send()
        to_cam(SUMS, cam_send.at[0], cam_sums, k).wait_send()

    each_cam(sent)
    to_frame(0).wait_send()
    to_frame(1).wait_send()

    def sent_node(k, carry):
        to_node(VISIBLE, visible_send, visible_recv, k, True).wait_send()
        to_node(RETURNS, returns_send, returns_recv, k, True).wait_send()
        to_node(NODE_SUMS, node_sums, node_sums, k, False).wait_send()
        return carry

    lax.fori_loop(1, node_count, sent_node, 0)


def solution(mesh):
    node_count, cam_count = mesh.shape["nodes"], mesh.shape["cams"]

    def on_device(iterate, residual, direction, precond, send_list, grads, node_refs, skin, rigid_nbr):
        local, params, width = direction.shape
        pixel_count = node_refs.shape[1]
        slots = send_list.shape[2]
        groups = cam_count // HALVES
        per_group = params // groups
        span = width // HALVES
        rows = per_group * span
        held = local * cam_count
        keys = slots * node_count
        tile = min(512, pixel_count)
        up = lambda size, to: (size + to - 1) // to * to
        side = up(max(rows, keys), 128)
        message = up(rows, 128)
        turn = lambda value: jnp.transpose(value, (1, 0, 2))
        f32, bf16 = jnp.float32, jnp.bfloat16
        slice_shape = (cam_count, per_group, local, width)
        dma = pltpu.SemaphoreType.DMA
        vmem = pl.BlockSpec(memory_space=pltpu.VMEM)
        patch_shape = jax.ShapeDtypeStruct((params, local, width), f32)
        outs = pl.pallas_call(
            functools.partial(kernel, node_count, cam_count, tile),
            out_shape=(patch_shape,) * 3,
            in_specs=[vmem] * 9,
            out_specs=[vmem] * 3,
            scratch_shapes=[
                pltpu.VMEM((cam_count, 8, pixel_count), f32),
                pltpu.VMEM((groups, per_group, pixel_count), f32),
                pltpu.VMEM((cam_count, per_group, pixel_count), f32),
                pltpu.VMEM((cam_count, keys, pixel_count), bf16),
                pltpu.VMEM((cam_count, span, pixel_count), f32),
                pltpu.VMEM(slice_shape, f32),
                pltpu.VMEM(slice_shape, f32),
                pltpu.VMEM(slice_shape, f32),
                pltpu.VMEM((params, local, width), f32),
                pltpu.VMEM(slice_shape, f32),
                pltpu.VMEM((2, params, local, width), f32),
                pltpu.VMEM((per_group, held, width), f32),
                pltpu.VMEM((per_group, held, width), f32),
                pltpu.VMEM((per_group, held, width), f32),
                pltpu.VMEM((per_group, held, width), f32),
                pltpu.VMEM((held, keys), f32),
                pltpu.VMEM((node_count, slots, message), f32),
                pltpu.VMEM((node_count, slots, message), f32),
                pltpu.VMEM((keys, 2 * rows), bf16),
                pltpu.VMEM((cam_count, 1, pixel_count), f32),
                pltpu.VMEM((cam_count, 1, pixel_count), f32),
                pltpu.VMEM((cam_count, 1, pixel_count), f32),
                pltpu.VMEM((2 * rows, keys), f32),
                pltpu.VMEM((side, side), f32),
                pltpu.VMEM((node_count, slots, message), f32),
                pltpu.VMEM((node_count, slots, message), f32),
                pltpu.VMEM(slice_shape, f32),
                pltpu.VMEM(slice_shape, f32),
                pltpu.VMEM((params, local, width), f32),
                pltpu.VMEM((node_count, 1, width), f32),
                pltpu.VMEM((cam_count, 1, width), f32),
                pltpu.VMEM((1, 1, width), f32),
                dma((10, cam_count)),
                dma((10, cam_count)),
                dma((3, node_count)),
                dma((3, node_count)),
                dma((2,)),
                dma((2,)),
            ],
            compiler_params=pltpu.CompilerParams(collective_id=0, has_side_effects=True, vmem_limit_bytes=60 << 20),
            name="cg_step",
        )(
            turn(iterate), turn(residual), turn(direction), turn(precond), jnp.transpose(send_list, (2, 0, 1)),
            grads, node_refs, skin, turn(rigid_nbr),
        )
        return tuple(turn(out) for out in outs)

    spec = P(("nodes", "cams"), None, None)
    split_last = P(None, ("nodes", "cams"))
    return jax.shard_map(
        on_device,
        mesh=mesh,
        in_specs=(spec, spec, spec, spec, P("nodes", None, None), split_last, split_last, split_last, spec),
        out_specs=(spec, spec, spec),
        check_vma=False,
    )
```

time: 523 us -> 91.5 us (0.17)
  blocking collectives: 217 us -> 0 us
  waiting for transfers between devices: 138 us -> 0 us
  Pallas kernels: 0 us -> 87.9 us
  other arithmetic: 57.4 us -> 0 us
  local copies, waits for them, and re-layouts: 57.4 us -> 2.63 us
  starting transfers between devices: 31.5 us -> 0 us
  between operations: 17.6 us -> 0.65 us
    psum x2 -> x0, blocking collectives: 196 us -> none  [the longest x1 103 us: on_device(): start_norm = lax.psum(jnp.sum(residual * scaled), ('nodes', 'cams'))]
    pallas_call x0 -> x1, Pallas kernels: none -> 87.9 us  [on_device(): pl.pallas_call(functools.partial(kernel, node_count, cam_count, tile), ou...]
    all_to_all x2 -> x0, waiting for transfers between devices: 70.3 us -> none  [the longest x1 38.7 us: on_device(): lax.all_to_all(outgoing, 'nodes', split_axis=1, concat_axis=1, tiled=True)]
    unnamed x2 -> x0, waiting for transfers between devices: 67.6 us -> none
    scatter-add x1 -> x0, other arithmetic: 49.6 us -> none  [on_device(): returns_local = jnp.zeros_like(visible).at[:, node_refs].add(scattered)]
    gather x1 -> x0, local copies, waits for them, and re-layouts: 32.3 us -> none  [on_device(): values = visible[:, node_refs]]
    all_to_all x2 -> x0, starting transfers between devices: 26.7 us -> none  [the longest x1 20.4 us: on_device(): lax.all_to_all(outgoing, 'nodes', split_axis=1, concat_axis=1, tiled=True)]
    all_gather x1 -> x0, blocking collectives: 20.6 us -> none  [on_device(): owned = lax.all_gather(direction, 'cams', axis=0, tiled=True)]
  transfers between devices with their start and end apart: 5 -> 0, of which waited for: 3 -> 0; matrix products, arithmetic and copies ran while one was open for 1% -> 0% of each run, Pallas kernels for 0% -> 0%
where the time goes in v1:
time: 91.5 us; the launch traced here: 91.1 us
  Pallas kernels  87.9 us (96%)
  local copies, waits for them, and re-layouts  2.63 us (3%)
    pallas_call x1, Pallas kernels, on_device(): pl.pallas_call(functools.partial(kernel, node_count, cam_count, tile), ou...  87.9 us
    unnamed x7, local copies, waits for them, and re-layouts  2.63 us

profile of v1, /device:TPU:1, one launch (start us, length us, event | category | flops | bytes accessed | tf_op | source)
XLA Modules:
  0.0 91.1 jit_solution(2591389772104451735)
XLA Ops:
  0.6 87.9 %cg_step.1 = (f32[12,2,128]{2,1,0:T(2,128)}, f32[12,2,128]{2,1,0:T(2,128)}, f32[12,2,128]{2,1,0:T(2,128)}) custom-call(f32[12,2,128]{2,1,0:T(2,128)} %bitcast.12, f32[12,2,128]{2,1,0:T(2,128)} %bitcast.13, f32[12,2,128]{2,1,0:T(2,128)} %bitcast.14, f32[12,2,128]{2,1,0:T(2,128)} %bitcast.15, s32[3,1,64]{2,1,0:T(1,128)} %bitcast.17, bf16[12,2048]{1,0:T(8,128)(2,1)} %grads.1, ...), custom_call_target="tpu_custom_call" | custom-call | tf_op jit(solution)/shard_map/cg_step/pallas_call | solution.py:426
  88.5 0.0 copy-start.1
  88.5 1.3 %copy.15 = f32[2,12,128]{2,0,1:T(2,128)} copy(f32[2,12,128]{2,0,1:T(2,128)} %bitcast.11) | data formatting | bytes 24576
  89.8 0.0 copy-done.1
  89.8 0.0 copy-start
  89.8 0.6 copy.16
  90.4 0.1 copy-done
  90.5 0.6 copy.17
Async XLA Ops:
  88.5 1.3 %copy-start.1 = (f32[12,2,128]{2,1,0:T(2,128)S(1)}, f32[12,2,128]{2,1,0:T(2,128)}, u32[]{:S(2)}) copy-start(f32[12,2,128]{2,1,0:T(2,128)} %get-tuple-element.7) | copy-start | bytes 36868
  89.8 0.7 copy-start

commit v2 on v1

--- a/solution.py
+++ b/solution.py
@@ -9,11 +9,12 @@
 
 MESH = pl.DeviceIdType.MESH
 FRAMES = 8
+TILES = (512, 1024, 2048)
 HALVES = 2
 temporal_weight = 0.5
 rigid_weight = 0.1
 
-OWNED, PIXELS, GRADS, RESID, PREC, SMOOTH, PARTIAL, TOTAL, IMAGE, SUMS = range(10)
+PIXELS, GRADS, TOTAL, OWNED, RESID, PREC, SMOOTH, PARTIAL, IMAGE, SUMS = range(10)
 VISIBLE, RETURNS, NODE_SUMS = range(3)
 
 
@@ -27,16 +28,17 @@
 
 
 def kernel(
-    node_count, cam_count, tile,
-    iterate, residual, direction, precond, send_list, grads, node_refs, skin, rigid_nbr,
-    new_iterate, new_residual, new_direction,
+    node_count, cam_count, tiles,
+    residual_in, direction_in, precond_in, send_list_in, grads_in, node_refs_in, skin_in, rigid_nbr_in,
+    image, factors,
+    residual, direction, precond, send_list, grads, node_refs, skin, rigid_nbr,
     pixels, grad_send, grad_rows, one_hot, weight,
     owned_recv, resid_recv, prec_recv, smooth_send, smooth_recv, frame_recv,
     owned, owned_resid, owned_prec, owned_smooth,
     chosen, visible_send, visible_recv, table, partial, partial_recv, total, returned, square,
-    returns_send, returns_recv, image_send, image_recv, image,
+    returns_send, returns_recv, image_send, image_recv,
     node_sums, cam_sums, cam_send,
-    cam_send_sem, cam_recv_sem, node_send_sem, node_recv_sem, frame_send_sem, frame_recv_sem,
+    cam_send_sem, cam_recv_sem, slot_sem, node_send_sem, node_recv_sem, frame_send_sem, frame_recv_sem, input_sem,
 ):
     me_node = lax.axis_index("nodes")
     me_cam = lax.axis_index("cams")
@@ -53,6 +55,14 @@
     first = group * per_group
     frame_step = node_count // FRAMES
 
+    pairs = (
+        (node_refs_in, node_refs), (skin_in, skin), (grads_in, grads), (direction_in, direction),
+        (residual_in, residual), (precond_in, precond), (send_list_in, send_list), (rigid_nbr_in, rigid_nbr),
+    )
+    inputs = [pltpu.make_async_copy(source, target, input_sem.at[i]) for i, (source, target) in enumerate(pairs)]
+    for copy in inputs:
+        copy.start()
+
     barrier = pltpu.get_barrier_semaphore()
 
     def greet_cam(k, carry):
@@ -70,14 +80,31 @@
         slot = lax.rem(cam_count - k, cam_count)
         return pltpu.make_async_remote_copy(
             src_ref=source, dst_ref=target.at[slot],
-            send_sem=cam_send_sem.at[phase, k], recv_sem=cam_recv_sem.at[phase, slot],
+            send_sem=cam_send_sem.at[phase], recv_sem=cam_recv_sem.at[phase],
             device_id={"cams": lax.rem(me_cam + k, cam_count)}, device_id_type=MESH,
         )
 
+    def from_cams(phase, target):
+        return pltpu.make_async_remote_copy(
+            src_ref=target.at[pl.ds(1, cam_count - 1)], dst_ref=target.at[pl.ds(1, cam_count - 1)],
+            send_sem=cam_send_sem.at[phase], recv_sem=cam_recv_sem.at[phase],
+            device_id={"cams": lax.rem(me_cam + 1, cam_count)}, device_id_type=MESH,
+        )
+
+    def to_cam_slot(phase, source, target, k, slot):
+        return pltpu.make_async_remote_copy(
+            src_ref=source, dst_ref=target.at[slot],
+            send_sem=cam_send_sem.at[phase], recv_sem=slot_sem.at[phase, slot],
+            device_id={"cams": lax.rem(me_cam + k, cam_count)}, device_id_type=MESH,
+        )
+
+    def to_cam_own(phase, source, target, k):
+        return to_cam_slot(phase, source, target, k, lax.rem(cam_count - k, cam_count))
+
     def from_cam(phase, target, k):
         return pltpu.make_async_remote_copy(
             src_ref=target.at[k], dst_ref=target.at[k],
-            send_sem=cam_send_sem.at[phase, k], recv_sem=cam_recv_sem.at[phase, k],
+            send_sem=cam_send_sem.at[phase], recv_sem=slot_sem.at[phase, k],
             device_id={"cams": lax.rem(me_cam + k, cam_count)}, device_id_type=MESH,
         )
 
@@ -85,27 +112,20 @@
         peer = lax.rem(me_node + k, node_count)
         return pltpu.make_async_remote_copy(
             src_ref=source.at[peer] if indexed else source.at[me_node], dst_ref=target.at[me_node],
-            send_sem=node_send_sem.at[phase, k], recv_sem=node_recv_sem.at[phase, me_node],
+            send_sem=node_send_sem.at[phase], recv_sem=node_recv_sem.at[phase],
             device_id={"nodes": peer}, device_id_type=MESH,
         )
 
-    def from_node(phase, target, k):
-        peer = lax.rem(me_node + k, node_count)
-        return pltpu.make_async_remote_copy(
-            src_ref=target.at[peer], dst_ref=target.at[peer],
-            send_sem=node_send_sem.at[phase, k], recv_sem=node_recv_sem.at[phase, peer],
-            device_id={"nodes": peer}, device_id_type=MESH,
+    def from_nodes(phase, target):
+        return pltpu.make_async_remote_copy(
+            src_ref=target.at[pl.ds(0, node_count - 1)], dst_ref=target.at[pl.ds(0, node_count - 1)],
+            send_sem=node_send_sem.at[phase], recv_sem=node_recv_sem.at[phase],
+            device_id={"nodes": lax.rem(me_node + 1, node_count)}, device_id_type=MESH,
         )
 
     def send_nodes(phase, source, target, indexed=True):
         def one(k, carry):
             to_node(phase, source, target, k, indexed).start()
-            return carry
-        lax.fori_loop(1, node_count, one, 0)
-
-    def wait_nodes(phase, target):
-        def one(k, carry):
-            from_node(phase, target, k).wait_recv()
             return carry
         lax.fori_loop(1, node_count, one, 0)
 
@@ -121,6 +141,8 @@
         else:
             lax.fori_loop(start, cam_count, one, 0)
 
+    for copy in inputs:
+        copy.wait()
     pixels[0, 0:4, :] = node_refs[...].astype(jnp.float32)
     pixels[0, 4:8, :] = skin[...].astype(jnp.float32)
     grad_all = grads[...].astype(jnp.float32)
@@ -154,11 +176,22 @@
     to_frame(0).start()
     to_frame(1).start()
 
-    def send_pixels(k):
-        to_cam(PIXELS, pixels.at[0], pixels, k).start()
-        to_cam(GRADS, grad_send.at[peer_group(k)], grad_rows, k).start()
-
-    each_cam(send_pixels)
+    down, up = cam_count // 2, (cam_count - 1) // 2
+
+    def relay(distance):
+        if 0 <= distance < down:
+            to_cam_slot(PIXELS, pixels.at[distance], pixels, cam_count - 1, distance + 1).start()
+        if -up < distance <= 0:
+            to_cam_slot(PIXELS, pixels.at[distance % cam_count], pixels, 1, cam_count + distance - 1).start()
+
+    def arrive(distance):
+        from_cam(PIXELS, pixels, distance % cam_count).wait_recv()
+        relay(distance)
+
+    relay(0)
+    each_cam(lambda k: to_cam_own(GRADS, grad_send.at[peer_group(k)], grad_rows, k).start())
+
+    tile = tiles[0]
 
     def build(k):
         def one(i, carry):
@@ -200,7 +233,7 @@
     def halves(target):
         return jnp.concatenate([take_half(target[f]) for f in range(per_group)], axis=1)
 
-    each_cam(lambda k: from_cam(OWNED, owned_recv, k).wait_recv())
+    from_cams(OWNED, owned_recv).wait_recv()
     gather_owned(owned_recv, owned)
     mine = halves(owned)
     one_hot_rows = chosen[...].astype(jnp.bfloat16)
@@ -210,6 +243,10 @@
         visible_send[:, j, 0:rows] = listed_rows[j * node_count:(j + 1) * node_count]
     visible_recv[pl.ds(me_node, 1)] = visible_send[pl.ds(me_node, 1)]
     send_nodes(VISIBLE, visible_send, visible_recv)
+    ring = [d for step in range(1, down + 1) for d in ((step, -step) if step <= up else (step,))]
+    for d in ring:
+        if abs(d) == 1:
+            arrive(d)
 
     each_cam(lambda k: to_cam(RESID, peer_params(residual, k), resid_recv, k).start())
     each_cam(lambda k: to_cam(PREC, peer_params(precond, k), prec_recv, k).start())
@@ -236,17 +273,22 @@
     smooth_recv[0] = smooth_send[pl.ds(first, per_group)]
     each_cam(lambda k: to_cam(SMOOTH, peer_params(smooth_send, k), smooth_recv, k).start())
 
-    def build_peer(k):
-        from_cam(PIXELS, pixels, k).wait_recv()
-        build(k)
-
-    each_cam(build_peer)
-
-    wait_nodes(VISIBLE, visible_recv)
+    for step in range(1, down + 1):
+        for d in ring:
+            if abs(d) == step + 1:
+                arrive(d)
+        for d in ring:
+            if abs(d) == step:
+                build(d % cam_count)
+
+    from_nodes(VISIBLE, visible_recv).wait_recv()
     for j in range(slots):
-        high, low = split(visible_recv[:, j, 0:rows])
-        table[j * node_count:(j + 1) * node_count, 0:rows] = high
-        table[j * node_count:(j + 1) * node_count, rows:2 * rows] = low
+        square[j * node_count:(j + 1) * node_count, 0:visible_recv.shape[2]] = visible_recv[:, j, :]
+    high, low = split(jnp.transpose(square[...])[0:rows, 0:keys])
+    table[0:rows] = high
+    table[rows:2 * rows] = low
+
+    project_tile = tiles[1]
 
     def project(k):
         @pl.when(k != 0)
@@ -254,16 +296,16 @@
             from_cam(GRADS, grad_rows, k).wait_recv()
 
         def one(i, carry):
-            at = pl.ds(pl.multiple_of(i * tile, tile), tile)
-            picked = dot(table[...], one_hot[k, :, at], ((0,), (0,)))
+            at = pl.ds(pl.multiple_of(i * project_tile, project_tile), project_tile)
+            picked = dot(table[...], one_hot[k, :, at], ((1,), (0,)))
             g = grad_rows[k, :, at]
-            summed = jnp.zeros((span, tile), jnp.float32)
+            summed = jnp.zeros((span, project_tile), jnp.float32)
             for f in range(per_group):
                 piece = picked[f * span:(f + 1) * span] + picked[rows + f * span:rows + (f + 1) * span]
                 summed = summed + piece * g[f:f + 1]
             partial[k, :, at] = jnp.sum(summed * weight[k, :, at], axis=0, keepdims=True)
             return carry
-        lax.fori_loop(0, pixel_count // tile, one, 0)
+        lax.fori_loop(0, pixel_count // project_tile, one, 0)
 
         @pl.when(k != 0)
         def _():
@@ -272,14 +314,16 @@
     each_cam(project, reverse=True, start=0)
 
     partial_recv[0] = partial[0]
-    each_cam(lambda k: from_cam(PARTIAL, partial_recv, k).wait_recv())
+    from_cams(PARTIAL, partial_recv).wait_recv()
     summed = partial_recv[0]
     for k in range(1, cam_count):
         summed = summed + partial_recv[k]
     total[0] = summed
-    each_cam(lambda k: to_cam(TOTAL, total.at[0], total, k).start(), reverse=True)
+    each_cam(lambda k: to_cam_own(TOTAL, total.at[0], total, k).start(), reverse=True)
 
     returned[...] = jnp.zeros_like(returned)
+
+    back_tile = tiles[2]
 
     def give_back(k):
         @pl.when(k != 0)
@@ -287,7 +331,7 @@
             from_cam(TOTAL, total, k).wait_recv()
 
         def one(i, carry):
-            at = pl.ds(pl.multiple_of(i * tile, tile), tile)
+            at = pl.ds(pl.multiple_of(i * back_tile, back_tile), back_tile)
             scaled = grad_rows[k, :, at] * total[k, :, at]
             w = weight[k, :, at]
             products = jnp.concatenate([w * scaled[f:f + 1] for f in range(per_group)], axis=0)
@@ -295,7 +339,7 @@
             both = jnp.concatenate([high, low], axis=0)
             returned[...] += dot(both, one_hot[k, :, at], ((1,), (1,)))
             return carry
-        lax.fori_loop(0, pixel_count // tile, one, 0)
+        lax.fori_loop(0, pixel_count // back_tile, one, 0)
 
     each_cam(give_back, start=0)
     square[...] = jnp.zeros_like(square)
@@ -307,9 +351,9 @@
     send_nodes(RETURNS, returns_send, returns_recv)
 
     start_norm = jnp.sum(residual[...] * precond[...] * residual[...], axis=(0, 1))[None]
-    each_cam(lambda k: from_cam(RESID, resid_recv, k).wait_recv())
-    each_cam(lambda k: from_cam(PREC, prec_recv, k).wait_recv())
-    each_cam(lambda k: from_cam(SMOOTH, smooth_recv, k).wait_recv())
+    from_cams(RESID, resid_recv).wait_recv()
+    from_cams(PREC, prec_recv).wait_recv()
+    from_cams(SMOOTH, smooth_recv).wait_recv()
     gather_owned(resid_recv, owned_resid)
     gather_owned(prec_recv, owned_prec)
     gather_owned(smooth_recv, owned_smooth)
@@ -317,7 +361,7 @@
     mine_prec = halves(owned_prec)
     weighted_resid = halves(owned_resid) * mine_prec
 
-    wait_nodes(RETURNS, returns_recv)
+    from_nodes(RETURNS, returns_recv).wait_recv()
     pieces = halves(owned_smooth)
     one_hot_rows = chosen[...].astype(jnp.bfloat16)
     for j in range(slots):
@@ -345,12 +389,12 @@
     image_recv[0] = image_send[0]
     each_cam(lambda k: to_cam(IMAGE, image_send.at[k], image_recv, k).start())
 
-    wait_nodes(NODE_SUMS, node_sums)
+    from_nodes(NODE_SUMS, node_sums).wait_recv()
     cam_send[0] = jnp.sum(node_sums[...], axis=0)
     cam_sums[0] = cam_send[0]
     each_cam(lambda k: to_cam(SUMS, cam_send.at[0], cam_sums, k).start())
 
-    each_cam(lambda k: from_cam(IMAGE, image_recv, k).wait_recv())
+    from_cams(IMAGE, image_recv).wait_recv()
     lane2 = lax.broadcasted_iota(jnp.int32, (local, width), 1)
     for g in range(params // per_group):
         for f in range(per_group):
@@ -359,7 +403,7 @@
             ]
             image[g * per_group + f] = jnp.where(lane2 < span, sides[0], sides[1])
 
-    each_cam(lambda k: from_cam(SUMS, cam_sums, k).wait_recv())
+    from_cams(SUMS, cam_sums).wait_recv()
     sums = jnp.sum(cam_sums[...], axis=0)
 
     def value_of(which):
@@ -369,35 +413,18 @@
     step = start / curvature
     new_norm = start - 2.0 * step * cross + step * step * square_norm
     ratio = new_norm / start
-    for f in range(params):
-        new_iterate[f] = iterate[f] + step * direction[f]
-        left = residual[f] - step * image[f]
-        new_residual[f] = left
-        new_direction[f] = precond[f] * left + ratio * direction[f]
-
-    def sent(k):
-        to_cam(OWNED, peer_params(direction, k), owned_recv, k).wait_send()
-        to_cam(PIXELS, pixels.at[0], pixels, k).wait_send()
-        to_cam(GRADS, grad_send.at[peer_group(k)], grad_rows, k).wait_send()
-        to_cam(RESID, peer_params(residual, k), resid_recv, k).wait_send()
-        to_cam(PREC, peer_params(precond, k), prec_recv, k).wait_send()
-        to_cam(SMOOTH, peer_params(smooth_send, k), smooth_recv, k).wait_send()
-        to_cam(PARTIAL, partial.at[k], partial_recv, k).wait_send()
-        to_cam(TOTAL, total.at[0], total, k).wait_send()
-        to_cam(IMAGE, image_send.at[k], image_recv, k).wait_send()
-        to_cam(SUMS, cam_send.at[0], cam_sums, k).wait_send()
-
-    each_cam(sent)
+    factors[0] = jnp.broadcast_to(step, (local, width))
+    factors[1] = jnp.broadcast_to(ratio, (local, width))
+
+    for phase, target in (
+        (PIXELS, pixels), (GRADS, grad_rows), (TOTAL, total), (OWNED, owned_recv), (RESID, resid_recv),
+        (PREC, prec_recv), (SMOOTH, smooth_recv), (PARTIAL, partial_recv), (IMAGE, image_recv), (SUMS, cam_sums),
+    ):
+        from_cams(phase, target).wait_send()
     to_frame(0).wait_send()
     to_frame(1).wait_send()
-
-    def sent_node(k, carry):
-        to_node(VISIBLE, visible_send, visible_recv, k, True).wait_send()
-        to_node(RETURNS, returns_send, returns_recv, k, True).wait_send()
-        to_node(NODE_SUMS, node_sums, node_sums, k, False).wait_send()
-        return carry
-
-    lax.fori_loop(1, node_count, sent_node, 0)
+    for phase, target in ((VISIBLE, visible_recv), (RETURNS, returns_recv), (NODE_SUMS, node_sums)):
+        from_nodes(phase, target).wait_send()
 
 
 def solution(mesh):
@@ -413,7 +440,7 @@
         rows = per_group * span
         held = local * cam_count
         keys = slots * node_count
-        tile = min(512, pixel_count)
+        tiles = tuple(min(size, pixel_count) for size in TILES)
         up = lambda size, to: (size + to - 1) // to * to
         side = up(max(rows, keys), 128)
         message = up(rows, 128)
@@ -423,12 +450,17 @@
         dma = pltpu.SemaphoreType.DMA
         vmem = pl.BlockSpec(memory_space=pltpu.VMEM)
         patch_shape = jax.ShapeDtypeStruct((params, local, width), f32)
-        outs = pl.pallas_call(
-            functools.partial(kernel, node_count, cam_count, tile),
-            out_shape=(patch_shape,) * 3,
-            in_specs=[vmem] * 9,
-            out_specs=[vmem] * 3,
+        inputs = (
+            turn(residual), turn(direction), turn(precond), jnp.transpose(send_list, (2, 0, 1)),
+            grads, node_refs, skin, turn(rigid_nbr),
+        )
+        image, factors = pl.pallas_call(
+            functools.partial(kernel, node_count, cam_count, tiles),
+            out_shape=(patch_shape, jax.ShapeDtypeStruct((2, local, width), f32)),
+            in_specs=[pl.BlockSpec(memory_space=pl.ANY)] * 8,
+            out_specs=[vmem] * 2,
             scratch_shapes=[
+                *(pltpu.VMEM(value.shape, value.dtype) for value in inputs),
                 pltpu.VMEM((cam_count, 8, pixel_count), f32),
                 pltpu.VMEM((groups, per_group, pixel_count), f32),
                 pltpu.VMEM((cam_count, per_group, pixel_count), f32),
@@ -447,7 +479,7 @@
                 pltpu.VMEM((held, keys), f32),
                 pltpu.VMEM((node_count, slots, message), f32),
                 pltpu.VMEM((node_count, slots, message), f32),
-                pltpu.VMEM((keys, 2 * rows), bf16),
+                pltpu.VMEM((2 * rows, keys), bf16),
                 pltpu.VMEM((cam_count, 1, pixel_count), f32),
                 pltpu.VMEM((cam_count, 1, pixel_count), f32),
                 pltpu.VMEM((cam_count, 1, pixel_count), f32),
@@ -457,24 +489,25 @@
                 pltpu.VMEM((node_count, slots, message), f32),
                 pltpu.VMEM(slice_shape, f32),
                 pltpu.VMEM(slice_shape, f32),
-                pltpu.VMEM((params, local, width), f32),
                 pltpu.VMEM((node_count, 1, width), f32),
                 pltpu.VMEM((cam_count, 1, width), f32),
                 pltpu.VMEM((1, 1, width), f32),
-                dma((10, cam_count)),
-                dma((10, cam_count)),
-                dma((3, node_count)),
-                dma((3, node_count)),
+                dma((10,)),
+                dma((10,)),
+                dma((3, cam_count)),
+                dma((3,)),
+                dma((3,)),
                 dma((2,)),
                 dma((2,)),
+                dma((8,)),
             ],
             compiler_params=pltpu.CompilerParams(collective_id=0, has_side_effects=True, vmem_limit_bytes=60 << 20),
             name="cg_step",
-        )(
-            turn(iterate), turn(residual), turn(direction), turn(precond), jnp.transpose(send_list, (2, 0, 1)),
-            grads, node_refs, skin, turn(rigid_nbr),
-        )
-        return tuple(turn(out) for out in outs)
+        )(*inputs)
+        image = turn(image)
+        step, ratio = factors[0][:, None, :], factors[1][:, None, :]
+        new_residual = residual - step * image
+        return iterate + step * direction, new_residual, precond * new_residual + ratio * direction
 
     spec = P(("nodes", "cams"), None, None)
     split_last = P(None, ("nodes", "cams"))

time: 91.5 us -> 75.5 us (0.83)
  Pallas kernels: 87.9 us -> 72.6 us
  local copies, waits for them, and re-layouts: 2.63 us -> 0.7 us
  other arithmetic: 0 us -> 1.33 us
    pallas_call x1, Pallas kernels: 87.9 us -> 72.6 us  [on_device(): pl.pallas_call(functools.partial(kernel, node_count, cam_count, tiles), o...]
    unnamed x7 -> x10, local copies, waits for them, and re-layouts: 2.63 us -> 0.7 us
    add x0 -> x1, other arithmetic: none -> 1.33 us  [on_device(): precond * new_residual + ratio * direction]
where the time goes in v2:
time: 75.5 us; the launch traced here: 75.3 us
  Pallas kernels  72.6 us (96%)
  other arithmetic  1.33 us (2%)
    pallas_call x1, Pallas kernels, on_device(): pl.pallas_call(functools.partial(kernel, node_count, cam_count, tiles), o...  72.6 us

profile of v2, /device:TPU:1, one launch (start us, length us, event | category | flops | bytes accessed | tf_op | source)
XLA Modules:
  0.0 75.3 jit_solution(9944756071635096447)
XLA Ops:
  0.6 0.0 copy-start
  0.6 0.0 copy-start.1
  0.7 0.0 copy-start.2
  0.7 0.0 copy-start.3
  0.7 72.6 %cg_step.1 = (f32[12,2,128]{2,1,0:T(2,128)}, f32[2,2,128]{2,1,0:T(2,128)}) custom-call(f32[12,2,128]{2,1,0:T(2,128)} %bitcast.14, f32[12,2,128]{2,1,0:T(2,128)} %bitcast.12, f32[12,2,128]{2,1,0:T(2,128)} %bitcast.13, s32[3,1,64]{2,1,0:T(1,128)} %bitcast.16, bf16[12,2048]{1,0:T(8,128)(2,1)} %grads_in.1, s32[4,2048]{1,0:T(4,128)} %node_refs_in.1, ...), custom_call_target="tpu_custom_call" | custom-call | tf_op jit(solution)/shard_map/cg_step/pallas_call | solution.py:457
  73.3 0.0 copy-start.4
  73.3 0.7 copy-done.4
  73.9 0.0 copy-done
  73.9 0.0 copy-done.1
  73.9 0.0 copy-done.2
  74.0 0.0 copy-done.3
  74.0 1.3 %multiply_add_fusion = (f32[2,12,128]{2,0,1:T(2,128)}, f32[2,12,128]{2,0,1:T(2,128)}, f32[2,12,128]{2,0,1:T(2,128)}) fusion(f32[2,12,128]{2,0,1:T(2,128)S(1)} %copy-done, f32[2,12,128]{2,0,1:T(2,128)S(1)} %copy-done.1, f32[2,128]{1,0:T(2,128)S(1)} %get-tuple-element.10, f32[2,12,128]{2,0,1:T(2,128)S(1)} %copy-done.2, f32[12,2,128]{2,1,0:T(2,128)} %get-tuple-element.6, ...), kind=kLoop, calls=%fused_computation.1 | loop fusion | flops 21504 | bytes 100352 | tf_op jit(solution)/shard_map/add | solution.py:510
  (1 shorter events, 0.0 us)
Async XLA Ops:
  0.6 73.3 %copy-start = (f32[2,12,128]{2,0,1:T(2,128)S(1)}, f32[2,12,128]{2,0,1:T(2,128)}, u32[]{:S(2)}) copy-start(f32[2,12,128]{2,0,1:T(2,128)} %param.11) | copy-start | bytes 36868
  0.6 73.3 %copy-start.1 = (f32[2,12,128]{2,0,1:T(2,128)S(1)}, f32[2,12,128]{2,0,1:T(2,128)}, u32[]{:S(2)}) copy-start(f32[2,12,128]{2,0,1:T(2,128)} %param.12) | copy-start | bytes 36868
  0.7 73.3 %copy-start.2 = (f32[2,12,128]{2,0,1:T(2,128)S(1)}, f32[2,12,128]{2,0,1:T(2,128)}, u32[]{:S(2)}) copy-start(f32[2,12,128]{2,0,1:T(2,128)} %param.10) | copy-start | bytes 36868
  0.7 73.3 %copy-start.3 = (f32[2,12,128]{2,0,1:T(2,128)S(1)}, f32[2,12,128]{2,0,1:T(2,128)}, u32[]{:S(2)}) copy-start(f32[2,12,128]{2,0,1:T(2,128)} %param.9) | copy-start | bytes 36868
  73.3 0.7 copy-start.4

commit v3 on v2

--- a/solution.py
+++ b/solution.py
@@ -9,12 +9,13 @@
 
 MESH = pl.DeviceIdType.MESH
 FRAMES = 8
+REACH = 2
 TILES = (512, 1024, 2048)
 HALVES = 2
 temporal_weight = 0.5
 rigid_weight = 0.1
 
-PIXELS, GRADS, TOTAL, OWNED, RESID, PREC, SMOOTH, PARTIAL, IMAGE, SUMS = range(10)
+PIXELS, GRADS, TOTAL, OWNED, REST, PARTIAL, IMAGE, SUMS = range(8)
 VISIBLE, RETURNS, NODE_SUMS = range(3)
 
 
@@ -33,7 +34,7 @@
     image, factors,
     residual, direction, precond, send_list, grads, node_refs, skin, rigid_nbr,
     pixels, grad_send, grad_rows, one_hot, weight,
-    owned_recv, resid_recv, prec_recv, smooth_send, smooth_recv, frame_recv,
+    owned_recv, rest_send, rest_recv, frame_recv,
     owned, owned_resid, owned_prec, owned_smooth,
     chosen, visible_send, visible_recv, table, partial, partial_recv, total, returned, square,
     returns_send, returns_recv, image_send, image_recv,
@@ -65,51 +66,73 @@
 
     barrier = pltpu.get_barrier_semaphore()
 
-    def greet_cam(k, carry):
-        pl.semaphore_signal(barrier, inc=1, device_id={"cams": lax.rem(me_cam + k, cam_count)}, device_id_type=MESH)
-        return carry
-
-    def greet_node(k, carry):
-        pl.semaphore_signal(barrier, inc=1, device_id={"nodes": lax.rem(me_node + k, node_count)}, device_id_type=MESH)
-        return carry
-
-    lax.fori_loop(1, cam_count, greet_cam, 0)
-    lax.fori_loop(1, node_count, greet_node, 0)
+    def wrap(value, size):
+        return jnp.where(value >= size, value - size, value)
+
+    def each_node(body):
+        middle = node_count // 2
+        body(middle)
+
+        def both(i, carry):
+            body(middle + i)
+            body(middle - i)
+            return carry
+
+        lax.fori_loop(1, middle, both, 0)
+
+    def cam_peer(k):
+        return wrap(me_cam + k, cam_count)
+
+    cam_peers = [me_cam] + [wrap(me_cam + k, cam_count) for k in range(1, cam_count)]
+    near_first = [k for d in range(1, cam_count // 2 + 1) for k in sorted({d, cam_count - d})]
+
+    def place(i):
+        return jnp.where(lax.rem(i, 2) == 1, (i + 1) // 2, cam_count - i // 2)
+
+    def each_cam(body):
+        for k in near_first:
+            body(k)
+
+    def greet(**place):
+        pl.semaphore_signal(barrier, inc=1, device_id=place, device_id_type=MESH)
+
+    each_node(lambda k: greet(nodes=wrap(me_node + k, node_count)))
+    each_cam(lambda k: greet(cams=cam_peers[k]))
 
     def to_cam(phase, source, target, k):
-        slot = lax.rem(cam_count - k, cam_count)
+        slot = cam_count - k
         return pltpu.make_async_remote_copy(
             src_ref=source, dst_ref=target.at[slot],
             send_sem=cam_send_sem.at[phase], recv_sem=cam_recv_sem.at[phase],
-            device_id={"cams": lax.rem(me_cam + k, cam_count)}, device_id_type=MESH,
+            device_id={"cams": cam_peer(k)}, device_id_type=MESH,
         )
 
     def from_cams(phase, target):
         return pltpu.make_async_remote_copy(
             src_ref=target.at[pl.ds(1, cam_count - 1)], dst_ref=target.at[pl.ds(1, cam_count - 1)],
             send_sem=cam_send_sem.at[phase], recv_sem=cam_recv_sem.at[phase],
-            device_id={"cams": lax.rem(me_cam + 1, cam_count)}, device_id_type=MESH,
+            device_id={"cams": cam_peers[1]}, device_id_type=MESH,
         )
 
     def to_cam_slot(phase, source, target, k, slot):
         return pltpu.make_async_remote_copy(
             src_ref=source, dst_ref=target.at[slot],
             send_sem=cam_send_sem.at[phase], recv_sem=slot_sem.at[phase, slot],
-            device_id={"cams": lax.rem(me_cam + k, cam_count)}, device_id_type=MESH,
+            device_id={"cams": cam_peer(k)}, device_id_type=MESH,
         )
 
     def to_cam_own(phase, source, target, k):
-        return to_cam_slot(phase, source, target, k, lax.rem(cam_count - k, cam_count))
+        return to_cam_slot(phase, source, target, k, cam_count - k)
 
     def from_cam(phase, target, k):
         return pltpu.make_async_remote_copy(
             src_ref=target.at[k], dst_ref=target.at[k],
             send_sem=cam_send_sem.at[phase], recv_sem=slot_sem.at[phase, k],
-            device_id={"cams": lax.rem(me_cam + k, cam_count)}, device_id_type=MESH,
+            device_id={"cams": cam_peer(k)}, device_id_type=MESH,
         )
 
     def to_node(phase, source, target, k, indexed):
-        peer = lax.rem(me_node + k, node_count)
+        peer = wrap(me_node + k, node_count)
         return pltpu.make_async_remote_copy(
             src_ref=source.at[peer] if indexed else source.at[me_node], dst_ref=target.at[me_node],
             send_sem=node_send_sem.at[phase], recv_sem=node_recv_sem.at[phase],
@@ -124,22 +147,7 @@
         )
 
     def send_nodes(phase, source, target, indexed=True):
-        def one(k, carry):
-            to_node(phase, source, target, k, indexed).start()
-            return carry
-        lax.fori_loop(1, node_count, one, 0)
-
-    def near(i):
-        return jnp.where(lax.rem(i, 2) == 1, (i + 1) // 2, lax.rem(cam_count - i // 2, cam_count))
-
-    def each_cam(body, reverse=False, start=1):
-        def one(i, carry):
-            body(near(cam_count - 1 - i if reverse else i))
-            return carry
-        if reverse:
-            lax.fori_loop(0, cam_count - start, one, 0)
-        else:
-            lax.fori_loop(start, cam_count, one, 0)
+        each_node(lambda k: to_node(phase, source, target, k, indexed).start())
 
     for copy in inputs:
         copy.wait()
@@ -149,16 +157,15 @@
     for g in range(params // per_group):
         grad_send[g] = grad_all[g * per_group:(g + 1) * per_group]
     grad_rows[0] = grad_send[group]
-    visible_send[...] = jnp.zeros_like(visible_send)
-    returns_send[...] = jnp.zeros_like(returns_send)
     owned_recv[0] = direction[pl.ds(first, per_group)]
-    resid_recv[0] = residual[pl.ds(first, per_group)]
-    prec_recv[0] = precond[pl.ds(first, per_group)]
+    for g in range(params // per_group):
+        rest_send[g, 0] = residual[g * per_group:(g + 1) * per_group]
+        rest_send[g, 1] = precond[g * per_group:(g + 1) * per_group]
 
     pl.semaphore_wait(barrier, cam_count - 1 + node_count - 1)
 
     def peer_group(k):
-        return lax.rem(me_cam + k, cam_count) // HALVES
+        return cam_peers[k] // HALVES
 
     def peer_params(source, k):
         return source.at[pl.ds(peer_group(k) * per_group, per_group)]
@@ -177,18 +184,22 @@
     to_frame(1).start()
 
     down, up = cam_count // 2, (cam_count - 1) // 2
-
-    def relay(distance):
-        if 0 <= distance < down:
-            to_cam_slot(PIXELS, pixels.at[distance], pixels, cam_count - 1, distance + 1).start()
-        if -up < distance <= 0:
-            to_cam_slot(PIXELS, pixels.at[distance % cam_count], pixels, 1, cam_count + distance - 1).start()
+    ring = [d for step in range(1, down + 1) for d in ((step, -step) if step <= up else (step,))]
+
+    def pass_on(have, want):
+        to_cam_slot(
+            PIXELS, pixels.at[have % cam_count], pixels, (have - want) % cam_count, want % cam_count
+        ).start()
 
     def arrive(distance):
         from_cam(PIXELS, pixels, distance % cam_count).wait_recv()
-        relay(distance)
-
-    relay(0)
+        for d in ring:
+            if abs(d) > REACH and distance == (REACH if d > 0 else -REACH):
+                pass_on(distance, d)
+
+    for d in ring:
+        if abs(d) <= REACH:
+            pass_on(0, d)
     each_cam(lambda k: to_cam_own(GRADS, grad_send.at[peer_group(k)], grad_rows, k).start())
 
     tile = tiles[0]
@@ -225,13 +236,37 @@
     def take_half(value):
         return jnp.where(half == 0, value[:, :span], value[:, span:])
 
-    def gather_owned(received, target):
+    def gather_owned(received, target, *which):
         for k in range(cam_count):
             for f in range(per_group):
-                target[f, k * local:(k + 1) * local, :] = received[k, f]
+                target[f, k * local:(k + 1) * local, :] = received[(k, *which, f)]
 
     def halves(target):
         return jnp.concatenate([take_half(target[f]) for f in range(per_group)], axis=1)
+
+    whole, odd = per_group // 2, per_group % 2
+
+    def pack(target, value):
+        for j in range(slots):
+            part = value[j * node_count:(j + 1) * node_count]
+            for p in range(whole):
+                target[:, j * whole + p, :] = part[:, p * width:(p + 1) * width]
+        if odd:
+            at = whole * width
+            last = [value[j * node_count:(j + 1) * node_count, at:at + span] for j in range(slots)]
+            last = last + [jnp.zeros_like(last[0])] * (slots % 2)
+            for i in range(0, slots, 2):
+                target[:, slots * whole + i // 2, :] = jnp.concatenate(last[i:i + 2], axis=1)
+
+    def unpack(target, source):
+        for j in range(slots):
+            at = pl.ds(j * node_count, node_count)
+            for p in range(whole):
+                target[at, p * width:(p + 1) * width] = source[:, j * whole + p, :]
+            if odd:
+                pair = source[:, slots * whole + j // 2, :]
+                side = span * (j % 2)
+                target[at, whole * width:whole * width + span] = pair[:, side:side + span]
 
     from_cams(OWNED, owned_recv).wait_recv()
     gather_owned(owned_recv, owned)
@@ -239,17 +274,72 @@
     one_hot_rows = chosen[...].astype(jnp.bfloat16)
     high, low = split(mine)
     listed_rows = dot(one_hot_rows, high, ((0,), (0,))) + dot(one_hot_rows, low, ((0,), (0,)))
-    for j in range(slots):
-        visible_send[:, j, 0:rows] = listed_rows[j * node_count:(j + 1) * node_count]
+    pack(visible_send, listed_rows)
     visible_recv[pl.ds(me_node, 1)] = visible_send[pl.ds(me_node, 1)]
     send_nodes(VISIBLE, visible_send, visible_recv)
-    ring = [d for step in range(1, down + 1) for d in ((step, -step) if step <= up else (step,))]
-    for d in ring:
-        if abs(d) == 1:
-            arrive(d)
-
-    each_cam(lambda k: to_cam(RESID, peer_params(residual, k), resid_recv, k).start())
-    each_cam(lambda k: to_cam(PREC, peer_params(precond, k), prec_recv, k).start())
+
+    near_count = len([d for d in ring if abs(d) <= REACH])
+    for d in ring[:near_count][::-1]:
+        arrive(d)
+
+    def build_near(i, carry):
+        build(place(i))
+        return carry
+
+    lax.fori_loop(1, near_count + 1, build_near, 0)
+
+    from_nodes(VISIBLE, visible_recv).wait_recv()
+    unpack(square, visible_recv)
+    high, low = split(jnp.transpose(square[...])[0:rows, 0:keys])
+    table[0:rows] = high
+    table[rows:2 * rows] = low
+
+    project_tile = tiles[1]
+
+    def project(k):
+        @pl.when(k != 0)
+        def _():
+            from_cam(GRADS, grad_rows, k).wait_recv()
+
+        def one(i, carry):
+            at = pl.ds(pl.multiple_of(i * project_tile, project_tile), project_tile)
+            picked = dot(table[...], one_hot[k, :, at], ((1,), (0,)))
+            g = grad_rows[k, :, at]
+            summed = jnp.zeros((span, project_tile), jnp.float32)
+            for f in range(per_group):
+                piece = picked[f * span:(f + 1) * span] + picked[rows + f * span:rows + (f + 1) * span]
+                summed = summed + piece * g[f:f + 1]
+            partial[k, :, at] = jnp.sum(summed * weight[k, :, at], axis=0, keepdims=True)
+            return carry
+        lax.fori_loop(0, pixel_count // project_tile, one, 0)
+
+        @pl.when(k != 0)
+        def _():
+            to_cam(PARTIAL, partial.at[k], partial_recv, k).start()
+
+    middle = [d % cam_count for d in ring[:near_count] if abs(d) > 1]
+    last = [d % cam_count for d in ring[near_count:]]
+    order = middle + last + [d % cam_count for d in ring if abs(d) == 1] + [0]
+
+    def in_order(i):
+        k = jnp.int32(order[0])
+        for at, which in enumerate(order):
+            k = jnp.where(i == at, which, k)
+        return k
+
+    def step_of(i, carry):
+        k = in_order(i)
+
+        @pl.when(jnp.logical_and(i >= len(middle), i < len(middle) + len(last)))
+        def _():
+            from_cam(PIXELS, pixels, k).wait_recv()
+            build(k)
+
+        project(k)
+        return carry
+
+    lax.fori_loop(0, cam_count, step_of, 0)
+
     to_frame(0).wait_recv()
     to_frame(1).wait_recv()
     ids = lax.broadcasted_iota(jnp.int32, (width, width), 0)
@@ -269,49 +359,9 @@
         for f in range(params):
             here = direction[f, q:q + 1, :]
             time = 2.0 * here - has_earlier * frame_recv[0, f, q:q + 1, :] - has_following * frame_recv[1, f, q:q + 1, :]
-            smooth_send[f, q:q + 1, :] = rigid_weight * rigid[f:f + 1] + temporal_weight * time
-    smooth_recv[0] = smooth_send[pl.ds(first, per_group)]
-    each_cam(lambda k: to_cam(SMOOTH, peer_params(smooth_send, k), smooth_recv, k).start())
-
-    for step in range(1, down + 1):
-        for d in ring:
-            if abs(d) == step + 1:
-                arrive(d)
-        for d in ring:
-            if abs(d) == step:
-                build(d % cam_count)
-
-    from_nodes(VISIBLE, visible_recv).wait_recv()
-    for j in range(slots):
-        square[j * node_count:(j + 1) * node_count, 0:visible_recv.shape[2]] = visible_recv[:, j, :]
-    high, low = split(jnp.transpose(square[...])[0:rows, 0:keys])
-    table[0:rows] = high
-    table[rows:2 * rows] = low
-
-    project_tile = tiles[1]
-
-    def project(k):
-        @pl.when(k != 0)
-        def _():
-            from_cam(GRADS, grad_rows, k).wait_recv()
-
-        def one(i, carry):
-            at = pl.ds(pl.multiple_of(i * project_tile, project_tile), project_tile)
-            picked = dot(table[...], one_hot[k, :, at], ((1,), (0,)))
-            g = grad_rows[k, :, at]
-            summed = jnp.zeros((span, project_tile), jnp.float32)
-            for f in range(per_group):
-                piece = picked[f * span:(f + 1) * span] + picked[rows + f * span:rows + (f + 1) * span]
-                summed = summed + piece * g[f:f + 1]
-            partial[k, :, at] = jnp.sum(summed * weight[k, :, at], axis=0, keepdims=True)
-            return carry
-        lax.fori_loop(0, pixel_count // project_tile, one, 0)
-
-        @pl.when(k != 0)
-        def _():
-            to_cam(PARTIAL, partial.at[k], partial_recv, k).start()
-
-    each_cam(project, reverse=True, start=0)
+            rest_send[f // per_group, 2, f % per_group, q:q + 1, :] = rigid_weight * rigid[f:f + 1] + temporal_weight * time
+    rest_recv[0] = rest_send[group]
+
 
     partial_recv[0] = partial[0]
     from_cams(PARTIAL, partial_recv).wait_recv()
@@ -319,7 +369,8 @@
     for k in range(1, cam_count):
         summed = summed + partial_recv[k]
     total[0] = summed
-    each_cam(lambda k: to_cam_own(TOTAL, total.at[0], total, k).start(), reverse=True)
+    for k in near_first[::-1]:
+        to_cam_own(TOTAL, total.at[0], total, k).start()
 
     returned[...] = jnp.zeros_like(returned)
 
@@ -341,33 +392,34 @@
             return carry
         lax.fori_loop(0, pixel_count // back_tile, one, 0)
 
-    each_cam(give_back, start=0)
+    each_cam(lambda k: to_cam(REST, rest_send.at[peer_group(k)], rest_recv, k).start())
+
+    def back_step(i, carry):
+        give_back(jnp.where(i == 0, 0, place(i)))
+        return carry
+
+    lax.fori_loop(0, cam_count, back_step, 0)
     square[...] = jnp.zeros_like(square)
     square[0:rows, 0:keys] = returned[0:rows] + returned[rows:2 * rows]
     by_key = jnp.transpose(square[...])
-    for j in range(slots):
-        returns_send[:, j, 0:rows] = by_key[j * node_count:(j + 1) * node_count, 0:rows]
+    pack(returns_send, by_key)
     returns_recv[pl.ds(me_node, 1)] = returns_send[pl.ds(me_node, 1)]
     send_nodes(RETURNS, returns_send, returns_recv)
 
     start_norm = jnp.sum(residual[...] * precond[...] * residual[...], axis=(0, 1))[None]
-    from_cams(RESID, resid_recv).wait_recv()
-    from_cams(PREC, prec_recv).wait_recv()
-    from_cams(SMOOTH, smooth_recv).wait_recv()
-    gather_owned(resid_recv, owned_resid)
-    gather_owned(prec_recv, owned_prec)
-    gather_owned(smooth_recv, owned_smooth)
+    from_cams(REST, rest_recv).wait_recv()
+    for which, target in enumerate((owned_resid, owned_prec, owned_smooth)):
+        gather_owned(rest_recv, target, which)
     mine = halves(owned)
     mine_prec = halves(owned_prec)
     weighted_resid = halves(owned_resid) * mine_prec
 
     from_nodes(RETURNS, returns_recv).wait_recv()
     pieces = halves(owned_smooth)
+    unpack(square, returns_recv)
     one_hot_rows = chosen[...].astype(jnp.bfloat16)
-    for j in range(slots):
-        high, low = split(returns_recv[:, j, 0:rows])
-        part = one_hot_rows[:, j * node_count:(j + 1) * node_count]
-        pieces = pieces + dot(part, high, ((1,), (0,))) + dot(part, low, ((1,), (0,)))
+    high, low = split(square[0:keys, 0:rows])
+    pieces = pieces + dot(one_hot_rows, high, ((1,), (0,))) + dot(one_hot_rows, low, ((1,), (0,)))
 
     lane = lax.broadcasted_iota(jnp.int32, (1, width), 1)
 
@@ -417,8 +469,8 @@
     factors[1] = jnp.broadcast_to(ratio, (local, width))
 
     for phase, target in (
-        (PIXELS, pixels), (GRADS, grad_rows), (TOTAL, total), (OWNED, owned_recv), (RESID, resid_recv),
-        (PREC, prec_recv), (SMOOTH, smooth_recv), (PARTIAL, partial_recv), (IMAGE, image_recv), (SUMS, cam_sums),
+        (PIXELS, pixels), (GRADS, grad_rows), (TOTAL, total), (OWNED, owned_recv), (REST, rest_recv),
+        (PARTIAL, partial_recv), (IMAGE, image_recv), (SUMS, cam_sums),
     ):
         from_cams(phase, target).wait_send()
     to_frame(0).wait_send()
@@ -443,7 +495,7 @@
         tiles = tuple(min(size, pixel_count) for size in TILES)
         up = lambda size, to: (size + to - 1) // to * to
         side = up(max(rows, keys), 128)
-        message = up(rows, 128)
+        message = slots * (per_group // 2) + (per_group % 2) * ((slots + 1) // 2)
         turn = lambda value: jnp.transpose(value, (1, 0, 2))
         f32, bf16 = jnp.float32, jnp.bfloat16
         slice_shape = (cam_count, per_group, local, width)
@@ -467,33 +519,31 @@
                 pltpu.VMEM((cam_count, keys, pixel_count), bf16),
                 pltpu.VMEM((cam_count, span, pixel_count), f32),
                 pltpu.VMEM(slice_shape, f32),
-                pltpu.VMEM(slice_shape, f32),
-                pltpu.VMEM(slice_shape, f32),
-                pltpu.VMEM((params, local, width), f32),
-                pltpu.VMEM(slice_shape, f32),
+                pltpu.VMEM((groups, 3, per_group, local, width), f32),
+                pltpu.VMEM((cam_count, 3, per_group, local, width), f32),
                 pltpu.VMEM((2, params, local, width), f32),
                 pltpu.VMEM((per_group, held, width), f32),
                 pltpu.VMEM((per_group, held, width), f32),
                 pltpu.VMEM((per_group, held, width), f32),
                 pltpu.VMEM((per_group, held, width), f32),
                 pltpu.VMEM((held, keys), f32),
-                pltpu.VMEM((node_count, slots, message), f32),
-                pltpu.VMEM((node_count, slots, message), f32),
+                pltpu.VMEM((node_count, message, width), f32),
+                pltpu.VMEM((node_count, message, width), f32),
                 pltpu.VMEM((2 * rows, keys), bf16),
                 pltpu.VMEM((cam_count, 1, pixel_count), f32),
                 pltpu.VMEM((cam_count, 1, pixel_count), f32),
                 pltpu.VMEM((cam_count, 1, pixel_count), f32),
                 pltpu.VMEM((2 * rows, keys), f32),
                 pltpu.VMEM((side, side), f32),
-                pltpu.VMEM((node_count, slots, message), f32),
-                pltpu.VMEM((node_count, slots, message), f32),
+                pltpu.VMEM((node_count, message, width), f32),
+                pltpu.VMEM((node_count, message, width), f32),
                 pltpu.VMEM(slice_shape, f32),
                 pltpu.VMEM(slice_shape, f32),
                 pltpu.VMEM((node_count, 1, width), f32),
                 pltpu.VMEM((cam_count, 1, width), f32),
                 pltpu.VMEM((1, 1, width), f32),
-                dma((10,)),
-                dma((10,)),
+                dma((8,)),
+                dma((8,)),
                 dma((3, cam_count)),
                 dma((3,)),
                 dma((3,)),

time: 75.5 us -> 68.9 us (0.913)
  Pallas kernels: 72.6 us -> 66 us
    pallas_call x1, Pallas kernels: 72.6 us -> 66 us  [on_device(): pl.pallas_call(functools.partial(kernel, node_count, cam_count, tiles), o...]
where the time goes in v3:
time: 68.9 us; the launch traced here: 68.7 us
  Pallas kernels  66 us (96%)
  other arithmetic  1.33 us (2%)
  local copies, waits for them, and re-layouts  0.7 us (1%)
  between operations  0.69 us (1%)
    pallas_call x1, Pallas kernels, on_device(): pl.pallas_call(functools.partial(kernel, node_count, cam_count, tiles), o...  66 us

profile of v3, /device:TPU:1, one launch (start us, length us, event | category | flops | bytes accessed | tf_op | source)
XLA Modules:
  0.0 68.7 jit_solution(5135587353339649925)
XLA Ops:
  0.6 0.0 copy-start
  0.6 0.0 copy-start.1
  0.7 0.0 copy-start.2
  0.7 0.0 copy-start.3
  0.7 66.0 %cg_step.1 = (f32[12,2,128]{2,1,0:T(2,128)}, f32[2,2,128]{2,1,0:T(2,128)}) custom-call(f32[12,2,128]{2,1,0:T(2,128)} %bitcast.14, f32[12,2,128]{2,1,0:T(2,128)} %bitcast.12, f32[12,2,128]{2,1,0:T(2,128)} %bitcast.13, s32[3,1,64]{2,1,0:T(1,128)} %bitcast.16, bf16[12,2048]{1,0:T(8,128)(2,1)} %grads_in.1, s32[4,2048]{1,0:T(4,128)} %node_refs_in.1, ...), custom_call_target="tpu_custom_call" | custom-call | tf_op jit(solution)/shard_map/cg_step/pallas_call | solution.py:509
  66.6 0.0 copy-start.4
  66.7 0.7 copy-done.4
  67.3 0.0 copy-done
  67.3 0.0 copy-done.1
  67.3 0.0 copy-done.2
  67.3 0.0 copy-done.3
  67.4 1.3 %multiply_add_fusion = (f32[2,12,128]{2,0,1:T(2,128)}, f32[2,12,128]{2,0,1:T(2,128)}, f32[2,12,128]{2,0,1:T(2,128)}) fusion(f32[2,12,128]{2,0,1:T(2,128)S(1)} %copy-done, f32[2,12,128]{2,0,1:T(2,128)S(1)} %copy-done.1, f32[2,128]{1,0:T(2,128)S(1)} %get-tuple-element.10, f32[2,12,128]{2,0,1:T(2,128)S(1)} %copy-done.2, f32[12,2,128]{2,1,0:T(2,128)} %get-tuple-element.6, ...), kind=kLoop, calls=%fused_computation.1 | loop fusion | flops 21504 | bytes 100352 | tf_op jit(solution)/shard_map/add | solution.py:560
  (1 shorter events, 0.0 us)
Async XLA Ops:
  0.6 66.7 %copy-start = (f32[2,12,128]{2,0,1:T(2,128)S(1)}, f32[2,12,128]{2,0,1:T(2,128)}, u32[]{:S(2)}) copy-start(f32[2,12,128]{2,0,1:T(2,128)} %param.11) | copy-start | bytes 36868
  0.6 66.7 %copy-start.1 = (f32[2,12,128]{2,0,1:T(2,128)S(1)}, f32[2,12,128]{2,0,1:T(2,128)}, u32[]{:S(2)}) copy-start(f32[2,12,128]{2,0,1:T(2,128)} %param.12) | copy-start | bytes 36868
  0.7 66.7 %copy-start.2 = (f32[2,12,128]{2,0,1:T(2,128)S(1)}, f32[2,12,128]{2,0,1:T(2,128)}, u32[]{:S(2)}) copy-start(f32[2,12,128]{2,0,1:T(2,128)} %param.10) | copy-start | bytes 36868
  0.7 66.7 %copy-start.3 = (f32[2,12,128]{2,0,1:T(2,128)S(1)}, f32[2,12,128]{2,0,1:T(2,128)}, u32[]{:S(2)}) copy-start(f32[2,12,128]{2,0,1:T(2,128)} %param.9) | copy-start | bytes 36868
  66.6 0.7 copy-start.4

commit v4 on v3

--- a/solution.py
+++ b/solution.py
@@ -10,12 +10,13 @@
 MESH = pl.DeviceIdType.MESH
 FRAMES = 8
 REACH = 2
-TILES = (512, 1024, 2048)
+TILES = (512, 1024)
+PARTS = 2
 HALVES = 2
 temporal_weight = 0.5
 rigid_weight = 0.1
 
-PIXELS, GRADS, TOTAL, OWNED, REST, PARTIAL, IMAGE, SUMS = range(8)
+PIXELS, GRADS, TOTAL, TOTAL_B, OWNED, REST, PARTIAL, PARTIAL_B, IMAGE, SUMS = range(10)
 VISIBLE, RETURNS, NODE_SUMS = range(3)
 
 
@@ -30,14 +31,14 @@
 
 def kernel(
     node_count, cam_count, tiles,
-    residual_in, direction_in, precond_in, send_list_in, grads_in, node_refs_in, skin_in, rigid_nbr_in,
-    image, factors,
-    residual, direction, precond, send_list, grads, node_refs, skin, rigid_nbr,
+    iterate_in, residual_in, direction_in, precond_in, send_list_in, grads_in, node_refs_in, skin_in, rigid_nbr_in,
+    result,
+    iterate, residual, direction, precond, send_list, grads, node_refs, skin, rigid_nbr,
     pixels, grad_send, grad_rows, one_hot, weight,
     owned_recv, rest_send, rest_recv, frame_recv,
     owned, owned_resid, owned_prec, owned_smooth,
     chosen, visible_send, visible_recv, table, partial, partial_recv, total, returned, square,
-    returns_send, returns_recv, image_send, image_recv,
+    returns_send, returns_recv, image_send, image_recv, image,
     node_sums, cam_sums, cam_send,
     cam_send_sem, cam_recv_sem, slot_sem, node_send_sem, node_recv_sem, frame_send_sem, frame_recv_sem, input_sem,
 ):
@@ -59,11 +60,9 @@
     pairs = (
         (node_refs_in, node_refs), (skin_in, skin), (grads_in, grads), (direction_in, direction),
         (residual_in, residual), (precond_in, precond), (send_list_in, send_list), (rigid_nbr_in, rigid_nbr),
+        (iterate_in, iterate),
     )
     inputs = [pltpu.make_async_copy(source, target, input_sem.at[i]) for i, (source, target) in enumerate(pairs)]
-    for copy in inputs:
-        copy.start()
-
     barrier = pltpu.get_barrier_semaphore()
 
     def wrap(value, size):
@@ -96,8 +95,10 @@
     def greet(**place):
         pl.semaphore_signal(barrier, inc=1, device_id=place, device_id_type=MESH)
 
+    each_cam(lambda k: greet(cams=cam_peers[k]))
+    for copy in inputs:
+        copy.start()
     each_node(lambda k: greet(nodes=wrap(me_node + k, node_count)))
-    each_cam(lambda k: greet(cams=cam_peers[k]))
 
     def to_cam(phase, source, target, k):
         slot = cam_count - k
@@ -183,24 +184,42 @@
     to_frame(0).start()
     to_frame(1).start()
 
-    down, up = cam_count // 2, (cam_count - 1) // 2
-    ring = [d for step in range(1, down + 1) for d in ((step, -step) if step <= up else (step,))]
-
-    def pass_on(have, want):
-        to_cam_slot(
-            PIXELS, pixels.at[have % cam_count], pixels, (have - want) % cam_count, want % cam_count
-        ).start()
+    opposite = cam_count // 2
+    ring = [d for step in range(1, opposite + 1) for d in ((step, -step) if step < opposite else (step,))]
+
+    def place_of(distance):
+        return distance % cam_count
+
+    def side(distance):
+        return jnp.where(half == 0, distance % cam_count, -distance % cam_count)
 
     def arrive(distance):
-        from_cam(PIXELS, pixels, distance % cam_count).wait_recv()
-        for d in ring:
-            if abs(d) > REACH and distance == (REACH if d > 0 else -REACH):
-                pass_on(distance, d)
-
-    for d in ring:
+        from_cam(PIXELS, pixels, place_of(distance)).wait_recv()
+        if abs(distance) == REACH:
+            on = distance + (1 if distance > 0 else -1)
+            if on in ring and abs(on) < opposite:
+                to_cam_slot(PIXELS, pixels.at[place_of(distance)], pixels, place_of(distance - on), place_of(on)).start()
+
+    def pass_opposite():
+        if REACH < opposite:
+            have = side(REACH)
+            to_cam_slot(PIXELS, pixels.at[have], pixels, side(REACH - opposite), opposite).start()
+
+    def send_grads(distance):
+        k = side(distance)
+        to_cam_slot(GRADS, grad_send.at[cam_peer(k) // HALVES], grad_rows, k, side(-distance)).start()
+
+    def pass_grads(distance):
+        have = side(-distance)
+        from_cam(GRADS, grad_rows, have).wait_recv()
+        to_cam_slot(GRADS, grad_rows.at[have], grad_rows, side(1), side(-distance - 1)).start()
+
+    for d in ring[::-1]:
         if abs(d) <= REACH:
-            pass_on(0, d)
-    each_cam(lambda k: to_cam_own(GRADS, grad_send.at[peer_group(k)], grad_rows, k).start())
+            to_cam_slot(PIXELS, pixels.at[0], pixels, place_of(-d), place_of(d)).start()
+    for j in range(opposite - 1, 0, -1):
+        send_grads(j if j % 2 == 0 else -j)
+    send_grads(1)
 
     tile = tiles[0]
 
@@ -281,65 +300,15 @@
     near_count = len([d for d in ring if abs(d) <= REACH])
     for d in ring[:near_count][::-1]:
         arrive(d)
-
+        if d == REACH:
+            pass_opposite()
     def build_near(i, carry):
         build(place(i))
         return carry
 
     lax.fori_loop(1, near_count + 1, build_near, 0)
-
-    from_nodes(VISIBLE, visible_recv).wait_recv()
-    unpack(square, visible_recv)
-    high, low = split(jnp.transpose(square[...])[0:rows, 0:keys])
-    table[0:rows] = high
-    table[rows:2 * rows] = low
-
-    project_tile = tiles[1]
-
-    def project(k):
-        @pl.when(k != 0)
-        def _():
-            from_cam(GRADS, grad_rows, k).wait_recv()
-
-        def one(i, carry):
-            at = pl.ds(pl.multiple_of(i * project_tile, project_tile), project_tile)
-            picked = dot(table[...], one_hot[k, :, at], ((1,), (0,)))
-            g = grad_rows[k, :, at]
-            summed = jnp.zeros((span, project_tile), jnp.float32)
-            for f in range(per_group):
-                piece = picked[f * span:(f + 1) * span] + picked[rows + f * span:rows + (f + 1) * span]
-                summed = summed + piece * g[f:f + 1]
-            partial[k, :, at] = jnp.sum(summed * weight[k, :, at], axis=0, keepdims=True)
-            return carry
-        lax.fori_loop(0, pixel_count // project_tile, one, 0)
-
-        @pl.when(k != 0)
-        def _():
-            to_cam(PARTIAL, partial.at[k], partial_recv, k).start()
-
-    middle = [d % cam_count for d in ring[:near_count] if abs(d) > 1]
-    last = [d % cam_count for d in ring[near_count:]]
-    order = middle + last + [d % cam_count for d in ring if abs(d) == 1] + [0]
-
-    def in_order(i):
-        k = jnp.int32(order[0])
-        for at, which in enumerate(order):
-            k = jnp.where(i == at, which, k)
-        return k
-
-    def step_of(i, carry):
-        k = in_order(i)
-
-        @pl.when(jnp.logical_and(i >= len(middle), i < len(middle) + len(last)))
-        def _():
-            from_cam(PIXELS, pixels, k).wait_recv()
-            build(k)
-
-        project(k)
-        return carry
-
-    lax.fori_loop(0, cam_count, step_of, 0)
-
+    for j in range(1, opposite):
+        pass_grads(j)
     to_frame(0).wait_recv()
     to_frame(1).wait_recv()
     ids = lax.broadcasted_iota(jnp.int32, (width, width), 0)
@@ -363,42 +332,120 @@
     rest_recv[0] = rest_send[group]
 
 
-    partial_recv[0] = partial[0]
-    from_cams(PARTIAL, partial_recv).wait_recv()
-    summed = partial_recv[0]
-    for k in range(1, cam_count):
-        summed = summed + partial_recv[k]
-    total[0] = summed
-    for k in near_first[::-1]:
-        to_cam_own(TOTAL, total.at[0], total, k).start()
-
+    def build_far(i, carry):
+        k = place(i)
+        from_cam(PIXELS, pixels, k).wait_recv()
+        build(k)
+        return carry
+
+    lax.fori_loop(near_count + 1, cam_count, build_far, 0)
+
+    from_nodes(VISIBLE, visible_recv).wait_recv()
+    unpack(square, visible_recv)
+    high, low = split(jnp.transpose(square[...])[0:rows, 0:keys])
+    table[0:rows] = high
+    table[rows:2 * rows] = low
+
+    piece_tile = tiles[1]
+    part_count = pixel_count // PARTS
+
+    def project(places, part):
+        def awaited(k):
+            @pl.when(jnp.logical_and(k != 0, jnp.where(half == 0, k <= opposite, k >= opposite)))
+            def _():
+                from_cam(GRADS, grad_rows, k).wait_recv()
+
+        def send(k):
+            @pl.when(k != 0)
+            def _():
+                to_cam(PARTIAL + part, partial.at[part, k], partial_recv.at[part], k).start()
+
+        if part == 0:
+            for k in places:
+                awaited(k)
+
+        def one(i, carry):
+            here = pl.ds(pl.multiple_of(i * piece_tile, piece_tile), piece_tile)
+            at = pl.ds(pl.multiple_of(part * part_count + i * piece_tile, piece_tile), piece_tile)
+            for k in places:
+                picked = dot(table[...], one_hot[k, :, at], ((1,), (0,)))
+                g = grad_rows[k, :, at]
+                summed = jnp.zeros((span, piece_tile), jnp.float32)
+                for f in range(per_group):
+                    piece = picked[f * span:(f + 1) * span] + picked[rows + f * span:rows + (f + 1) * span]
+                    summed = summed + piece * g[f:f + 1]
+                partial[part, k, :, here] = jnp.sum(summed * weight[k, :, at], axis=0, keepdims=True)
+            return carry
+        lax.fori_loop(0, part_count // piece_tile, one, 0)
+        for k in places:
+            send(k)
+
+    def sum_up(part):
+        partial_recv[part, 0] = partial[part, 0]
+        from_cams(PARTIAL + part, partial_recv.at[part]).wait_recv()
+        summed = partial_recv[part, 0]
+        for k in range(1, cam_count):
+            summed = summed + partial_recv[part, k]
+        total[part, 0] = summed
+        for k in near_first[::-1]:
+            to_cam_own(TOTAL + part, total.at[part, 0], total.at[part], k).start()
+
+    def give_back(places, part):
+        def awaited(k):
+            @pl.when(k != 0)
+            def _():
+                from_cam(TOTAL + part, total.at[part], k).wait_recv()
+
+        for k in places:
+            awaited(k)
+
+        def one(i, carry):
+            here = pl.ds(pl.multiple_of(i * piece_tile, piece_tile), piece_tile)
+            at = pl.ds(pl.multiple_of(part * part_count + i * piece_tile, piece_tile), piece_tile)
+            summed = returned[...]
+            for k in places:
+                scaled = grad_rows[k, :, at] * total[part, k, :, here]
+                w = weight[k, :, at]
+                products = jnp.concatenate([w * scaled[f:f + 1] for f in range(per_group)], axis=0)
+                high, low = split(products)
+                both = jnp.concatenate([high, low], axis=0)
+                summed = summed + dot(both, one_hot[k, :, at], ((1,), (1,)))
+            returned[...] = summed
+            return carry
+        lax.fori_loop(0, part_count // piece_tile, one, 0)
+
+    def listed(i, places):
+        k = jnp.int32(places[0])
+        for at, which in enumerate(places):
+            k = jnp.where(i == at, which, k)
+        return k
+
+    out_order = near_first[::-1] + [0]
+    back_order = [0] + near_first
+
+    def project_some(start, stop, part):
+        def one(i, carry):
+            project([listed(i, out_order[0::2]), listed(i, out_order[1::2])], part)
+            return carry
+        lax.fori_loop(start, stop, one, 0)
+
+    def give_back_some(start, stop, part):
+        def one(i, carry):
+            give_back([listed(i, back_order[0::2]), listed(i, back_order[1::2])], part)
+            return carry
+        lax.fori_loop(start, stop, one, 0)
+
+    pairs_count = cam_count // 2
+    late_sum = 1
+    project_some(0, pairs_count, 0)
+    project_some(0, pairs_count, 1)
+    sum_up(0)
     returned[...] = jnp.zeros_like(returned)
-
-    back_tile = tiles[2]
-
-    def give_back(k):
-        @pl.when(k != 0)
-        def _():
-            from_cam(TOTAL, total, k).wait_recv()
-
-        def one(i, carry):
-            at = pl.ds(pl.multiple_of(i * back_tile, back_tile), back_tile)
-            scaled = grad_rows[k, :, at] * total[k, :, at]
-            w = weight[k, :, at]
-            products = jnp.concatenate([w * scaled[f:f + 1] for f in range(per_group)], axis=0)
-            high, low = split(products)
-            both = jnp.concatenate([high, low], axis=0)
-            returned[...] += dot(both, one_hot[k, :, at], ((1,), (1,)))
-            return carry
-        lax.fori_loop(0, pixel_count // back_tile, one, 0)
-
     each_cam(lambda k: to_cam(REST, rest_send.at[peer_group(k)], rest_recv, k).start())
-
-    def back_step(i, carry):
-        give_back(jnp.where(i == 0, 0, place(i)))
-        return carry
-
-    lax.fori_loop(0, cam_count, back_step, 0)
+    give_back_some(0, late_sum, 0)
+    sum_up(1)
+    give_back_some(late_sum, pairs_count, 0)
+    give_back_some(0, pairs_count, 1)
     square[...] = jnp.zeros_like(square)
     square[0:rows, 0:keys] = returned[0:rows] + returned[rows:2 * rows]
     by_key = jnp.transpose(square[...])
@@ -465,14 +512,20 @@
     step = start / curvature
     new_norm = start - 2.0 * step * cross + step * step * square_norm
     ratio = new_norm / start
-    factors[0] = jnp.broadcast_to(step, (local, width))
-    factors[1] = jnp.broadcast_to(ratio, (local, width))
+    for f in range(params):
+        left = residual[f] - step * image[f]
+        result[f] = iterate[f] + step * direction[f]
+        result[params + f] = left
+        result[2 * params + f] = precond[f] * left + ratio * direction[f]
 
     for phase, target in (
-        (PIXELS, pixels), (GRADS, grad_rows), (TOTAL, total), (OWNED, owned_recv), (REST, rest_recv),
-        (PARTIAL, partial_recv), (IMAGE, image_recv), (SUMS, cam_sums),
+        (PIXELS, pixels), (GRADS, grad_rows), (OWNED, owned_recv), (REST, rest_recv),
+        (IMAGE, image_recv), (SUMS, cam_sums),
     ):
         from_cams(phase, target).wait_send()
+    for part in range(PARTS):
+        from_cams(TOTAL + part, total.at[part]).wait_send()
+        from_cams(PARTIAL + part, partial_recv.at[part]).wait_send()
     to_frame(0).wait_send()
     to_frame(1).wait_send()
     for phase, target in ((VISIBLE, visible_recv), (RETURNS, returns_recv), (NODE_SUMS, node_sums)):
@@ -492,7 +545,8 @@
         rows = per_group * span
         held = local * cam_count
         keys = slots * node_count
-        tiles = tuple(min(size, pixel_count) for size in TILES)
+        part_count = pixel_count // PARTS
+        tiles = (min(TILES[0], pixel_count), min(TILES[1], part_count))
         up = lambda size, to: (size + to - 1) // to * to
         side = up(max(rows, keys), 128)
         message = slots * (per_group // 2) + (per_group % 2) * ((slots + 1) // 2)
@@ -501,16 +555,15 @@
         slice_shape = (cam_count, per_group, local, width)
         dma = pltpu.SemaphoreType.DMA
         vmem = pl.BlockSpec(memory_space=pltpu.VMEM)
-        patch_shape = jax.ShapeDtypeStruct((params, local, width), f32)
         inputs = (
-            turn(residual), turn(direction), turn(precond), jnp.transpose(send_list, (2, 0, 1)),
+            turn(iterate), turn(residual), turn(direction), turn(precond), jnp.transpose(send_list, (2, 0, 1)),
             grads, node_refs, skin, turn(rigid_nbr),
         )
-        image, factors = pl.pallas_call(
+        result = pl.pallas_call(
             functools.partial(kernel, node_count, cam_count, tiles),
-            out_shape=(patch_shape, jax.ShapeDtypeStruct((2, local, width), f32)),
-            in_specs=[pl.BlockSpec(memory_space=pl.ANY)] * 8,
-            out_specs=[vmem] * 2,
+            out_shape=jax.ShapeDtypeStruct((3 * params, local, width), f32),
+            in_specs=[pl.BlockSpec(memory_space=pl.ANY)] * 9,
+            out_specs=vmem,
             scratch_shapes=[
                 *(pltpu.VMEM(value.shape, value.dtype) for value in inputs),
                 pltpu.VMEM((cam_count, 8, pixel_count), f32),
@@ -530,34 +583,32 @@
                 pltpu.VMEM((node_count, message, width), f32),
                 pltpu.VMEM((node_count, message, width), f32),
                 pltpu.VMEM((2 * rows, keys), bf16),
-                pltpu.VMEM((cam_count, 1, pixel_count), f32),
-                pltpu.VMEM((cam_count, 1, pixel_count), f32),
-                pltpu.VMEM((cam_count, 1, pixel_count), f32),
+                pltpu.VMEM((PARTS, cam_count, 1, part_count), f32),
+                pltpu.VMEM((PARTS, cam_count, 1, part_count), f32),
+                pltpu.VMEM((PARTS, cam_count, 1, part_count), f32),
                 pltpu.VMEM((2 * rows, keys), f32),
                 pltpu.VMEM((side, side), f32),
                 pltpu.VMEM((node_count, message, width), f32),
                 pltpu.VMEM((node_count, message, width), f32),
                 pltpu.VMEM(slice_shape, f32),
                 pltpu.VMEM(slice_shape, f32),
+                pltpu.VMEM((params, local, width), f32),
                 pltpu.VMEM((node_count, 1, width), f32),
                 pltpu.VMEM((cam_count, 1, width), f32),
                 pltpu.VMEM((1, 1, width), f32),
-                dma((8,)),
-                dma((8,)),
-                dma((3, cam_count)),
+                dma((10,)),
+                dma((10,)),
+                dma((4, cam_count)),
                 dma((3,)),
                 dma((3,)),
                 dma((2,)),
                 dma((2,)),
-                dma((8,)),
+                dma((9,)),
             ],
             compiler_params=pltpu.CompilerParams(collective_id=0, has_side_effects=True, vmem_limit_bytes=60 << 20),
             name="cg_step",
         )(*inputs)
-        image = turn(image)
-        step, ratio = factors[0][:, None, :], factors[1][:, None, :]
-        new_residual = residual - step * image
-        return iterate + step * direction, new_residual, precond * new_residual + ratio * direction
+        return tuple(turn(result[i * params:(i + 1) * params]) for i in range(3))
 
     spec = P(("nodes", "cams"), None, None)
     split_last = P(None, ("nodes", "cams"))

time: 68.9 us -> 66.5 us (0.965)
  Pallas kernels: 66 us -> 64.3 us
  other arithmetic: 1.33 us -> 0 us
    pallas_call x1, Pallas kernels: 66 us -> 64.3 us  [on_device(): pl.pallas_call(functools.partial(kernel, node_count, cam_count, tiles), o...]
    transpose x0 -> x1, local copies, waits for them, and re-layouts: none -> 1.35 us  [on_device(): turn = lambda value: jnp.transpose(value, (1, 0, 2))]
    add x1 -> x0, other arithmetic: 1.33 us -> none  [on_device(): precond * new_residual + ratio * direction]
    unnamed x10 -> x0, local copies, waits for them, and re-layouts: 0.7 us -> none
where the time goes in v4:
time: 66.5 us; the launch traced here: 66.3 us
  Pallas kernels  64.3 us (97%)
  local copies, waits for them, and re-layouts  1.35 us (2%)
    pallas_call x1, Pallas kernels, on_device(): pl.pallas_call(functools.partial(kernel, node_count, cam_count, tiles), o...  64.3 us
    transpose x1, local copies, waits for them, and re-layouts, on_device(): turn = lambda value: jnp.transpose(value, (1, 0, 2))  1.35 us

profile of v4, /device:TPU:1, one launch (start us, length us, event | category | flops | bytes accessed | tf_op | source)
XLA Modules:
  0.0 66.3 jit_solution(1609703311580912933)
XLA Ops:
  0.6 64.3 %cg_step.1 = f32[36,2,128]{2,1,0:T(2,128)} custom-call(f32[12,2,128]{2,1,0:T(2,128)} %bitcast.12, f32[12,2,128]{2,1,0:T(2,128)} %bitcast.13, f32[12,2,128]{2,1,0:T(2,128)} %bitcast.14, f32[12,2,128]{2,1,0:T(2,128)} %bitcast.15, s32[3,1,64]{2,1,0:T(1,128)} %bitcast.17, bf16[12,2048]{1,0:T(8,128)(2,1)} %grads_in.1, s32[4,2048]{1,0:T(4,128)} %node_refs_in.1, ...), custom_call_target="tpu_custom_call" | custom-call | tf_op jit(solution)/shard_map/cg_step/pallas_call | solution.py:562
  64.9 1.4 %slice_bitcast_fusion = (f32[2,12,128]{2,0,1:T(2,128)}, f32[2,12,128]{2,0,1:T(2,128)}, f32[2,12,128]{2,0,1:T(2,128)}) fusion(f32[36,2,128]{2,1,0:T(2,128)} %cg_step.1), kind=kLoop, calls=%fused_computation | loop fusion | bytes 73728 | tf_op jit(solution)/shard_map/transpose | solution.py:553

commit v5 on v4

--- a/solution.py
+++ b/solution.py
@@ -16,7 +16,7 @@
 temporal_weight = 0.5
 rigid_weight = 0.1
 
-PIXELS, GRADS, TOTAL, TOTAL_B, OWNED, REST, PARTIAL, PARTIAL_B, IMAGE, SUMS = range(10)
+PIXELS, PIXELS_B, GRADS, GRADS_B, TOTAL, TOTAL_B, OWNED, REST, PARTIAL, PARTIAL_B, IMAGE, SUMS = range(12)
 VISIBLE, RETURNS, NODE_SUMS = range(3)
 
 
@@ -48,7 +48,7 @@
     half = lax.rem(me_cam, HALVES)
     params, local, width = direction.shape
     slots = send_list.shape[0]
-    per_group = grad_send.shape[1]
+    per_group = grad_send.shape[2]
     span = width // HALVES
     rows = per_group * span
     keys = slots * node_count
@@ -152,16 +152,19 @@
 
     for copy in inputs:
         copy.wait()
-    pixels[0, 0:4, :] = node_refs[...].astype(jnp.float32)
-    pixels[0, 4:8, :] = skin[...].astype(jnp.float32)
+    part_count = pixel_count // PARTS
     grad_all = grads[...].astype(jnp.float32)
-    for g in range(params // per_group):
-        grad_send[g] = grad_all[g * per_group:(g + 1) * per_group]
-    grad_rows[0] = grad_send[group]
-    owned_recv[0] = direction[pl.ds(first, per_group)]
+    for part in range(PARTS):
+        columns = slice(part * part_count, (part + 1) * part_count)
+        pixels[part, 0, 0:4, :] = node_refs[:, columns].astype(jnp.float32)
+        pixels[part, 0, 4:8, :] = skin[:, columns].astype(jnp.float32)
+        for g in range(params // per_group):
+            grad_send[part, g] = grad_all[g * per_group:(g + 1) * per_group, columns]
+        grad_rows[part, 0] = grad_send[part, group]
     for g in range(params // per_group):
         rest_send[g, 0] = residual[g * per_group:(g + 1) * per_group]
         rest_send[g, 1] = precond[g * per_group:(g + 1) * per_group]
+    owned_recv[0] = direction[pl.ds(first, per_group)]
 
     pl.semaphore_wait(barrier, cam_count - 1 + node_count - 1)
 
@@ -193,40 +196,55 @@
     def side(distance):
         return jnp.where(half == 0, distance % cam_count, -distance % cam_count)
 
-    def arrive(distance):
-        from_cam(PIXELS, pixels, place_of(distance)).wait_recv()
-        if abs(distance) == REACH:
-            on = distance + (1 if distance > 0 else -1)
-            if on in ring and abs(on) < opposite:
-                to_cam_slot(PIXELS, pixels.at[place_of(distance)], pixels, place_of(distance - on), place_of(on)).start()
-
-    def pass_opposite():
+    def arrive(distance, part):
+        from_cam(PIXELS + part, pixels.at[part], place_of(distance)).wait_recv()
+        on = distance + (1 if distance > 0 else -1)
+        if abs(distance) == REACH and abs(on) < opposite:
+            to_cam_slot(
+                PIXELS + part, pixels.at[part, place_of(distance)], pixels.at[part], place_of(distance - on), place_of(on)
+            ).start()
+
+    def pass_opposite(part):
         if REACH < opposite:
             have = side(REACH)
-            to_cam_slot(PIXELS, pixels.at[have], pixels, side(REACH - opposite), opposite).start()
-
-    def send_grads(distance):
+            to_cam_slot(PIXELS + part, pixels.at[part, have], pixels.at[part], side(REACH - opposite), opposite).start()
+
+    def send_grads(distance, part):
         k = side(distance)
-        to_cam_slot(GRADS, grad_send.at[cam_peer(k) // HALVES], grad_rows, k, side(-distance)).start()
-
-    def pass_grads(distance):
+        source = grad_send.at[part, cam_peer(k) // HALVES]
+        to_cam_slot(GRADS + part, source, grad_rows.at[part], k, side(-distance)).start()
+
+    def pass_grads(distance, part):
         have = side(-distance)
-        from_cam(GRADS, grad_rows, have).wait_recv()
-        to_cam_slot(GRADS, grad_rows.at[have], grad_rows, side(1), side(-distance - 1)).start()
-
-    for d in ring[::-1]:
-        if abs(d) <= REACH:
-            to_cam_slot(PIXELS, pixels.at[0], pixels, place_of(-d), place_of(d)).start()
-    for j in range(opposite - 1, 0, -1):
-        send_grads(j if j % 2 == 0 else -j)
-    send_grads(1)
+        from_cam(GRADS + part, grad_rows.at[part], have).wait_recv()
+        to_cam_slot(GRADS + part, grad_rows.at[part, have], grad_rows.at[part], side(1), side(-distance - 1)).start()
+
+    def send_pixels(part):
+        for d in ring[::-1]:
+            if abs(d) <= REACH:
+                to_cam_slot(PIXELS + part, pixels.at[part, 0], pixels.at[part], place_of(-d), place_of(d)).start()
+        for j in range(opposite - 1, 0, -1):
+            send_grads(j if j % 2 == 0 else -j, part)
+        send_grads(1, part)
+
+    near_ring = [d for d in ring if abs(d) <= REACH]
+
+    def pass_pixels(part):
+        for d in near_ring[::-1]:
+            arrive(d, part)
+            if d == REACH:
+                pass_opposite(part)
+
+    send_pixels(0)
+    send_pixels(1)
 
     tile = tiles[0]
 
-    def build(k):
+    def build(k, part):
         def one(i, carry):
-            at = pl.ds(pl.multiple_of(i * tile, tile), tile)
-            block = pixels[k, :, at]
+            here = pl.ds(pl.multiple_of(i * tile, tile), tile)
+            at = pl.ds(pl.multiple_of(part * part_count + i * tile, tile), tile)
+            block = pixels[part, k, :, here]
             refs = block[0:4].astype(jnp.int32)
             weights = block[4:8]
             place = refs[0:1] >> 7
@@ -241,9 +259,10 @@
                 summed = summed + jnp.where(ids == within[s:s + 1], weights[s:s + 1], 0.0)
             weight[k, :, at] = summed
             return carry
-        lax.fori_loop(0, pixel_count // tile, one, 0)
-
-    build(0)
+        lax.fori_loop(0, part_count // tile, one, 0)
+
+    for part in range(PARTS):
+        build(0, part)
 
     wanted = lax.broadcasted_iota(jnp.int32, (held, node_count), 0)
     for j in range(slots):
@@ -297,18 +316,132 @@
     visible_recv[pl.ds(me_node, 1)] = visible_send[pl.ds(me_node, 1)]
     send_nodes(VISIBLE, visible_send, visible_recv)
 
-    near_count = len([d for d in ring if abs(d) <= REACH])
-    for d in ring[:near_count][::-1]:
-        arrive(d)
-        if d == REACH:
-            pass_opposite()
-    def build_near(i, carry):
-        build(place(i))
-        return carry
-
-    lax.fori_loop(1, near_count + 1, build_near, 0)
+    near_count = len(near_ring)
+
+    def build_near(part):
+        def one(i, carry):
+            build(place(i), part)
+            return carry
+        lax.fori_loop(1, near_count + 1, one, 0)
+
+    def build_far(part):
+        def one(i, carry):
+            k = place(i)
+            from_cam(PIXELS + part, pixels.at[part], k).wait_recv()
+            build(k, part)
+            return carry
+        lax.fori_loop(near_count + 1, cam_count, one, 0)
+
+    pass_pixels(0)
+    build_near(0)
     for j in range(1, opposite):
-        pass_grads(j)
+        pass_grads(j, 0)
+    pass_pixels(1)
+    build_near(1)
+    for j in range(1, opposite):
+        pass_grads(j, 1)
+    build_far(0)
+
+    from_nodes(VISIBLE, visible_recv).wait_recv()
+    unpack(square, visible_recv)
+    high, low = split(jnp.transpose(square[...])[0:rows, 0:keys])
+    table[0:rows] = high
+    table[rows:2 * rows] = low
+
+    piece_tile = tiles[1]
+
+    def project(places, part):
+        def awaited(k):
+            @pl.when(jnp.logical_and(k != 0, jnp.where(half == 0, k <= opposite, k >= opposite)))
+            def _():
+                from_cam(GRADS + part, grad_rows.at[part], k).wait_recv()
+
+        def send(k):
+            @pl.when(k != 0)
+            def _():
+                to_cam(PARTIAL + part, partial.at[part, k], partial_recv.at[part], k).start()
+
+        for k in places:
+            awaited(k)
+
+        def one(i, carry):
+            here = pl.ds(pl.multiple_of(i * piece_tile, piece_tile), piece_tile)
+            at = pl.ds(pl.multiple_of(part * part_count + i * piece_tile, piece_tile), piece_tile)
+            for k in places:
+                picked = dot(table[...], one_hot[k, :, at], ((1,), (0,)))
+                g = grad_rows[part, k, :, here]
+                summed = jnp.zeros((span, piece_tile), jnp.float32)
+                for f in range(per_group):
+                    piece = picked[f * span:(f + 1) * span] + picked[rows + f * span:rows + (f + 1) * span]
+                    summed = summed + piece * g[f:f + 1]
+                partial[part, k, :, here] = jnp.sum(summed * weight[k, :, at], axis=0, keepdims=True)
+            return carry
+        lax.fori_loop(0, part_count // piece_tile, one, 0)
+        for k in places:
+            send(k)
+
+    def sum_up(part):
+        partial_recv[part, 0] = partial[part, 0]
+        from_cams(PARTIAL + part, partial_recv.at[part]).wait_recv()
+        summed = partial_recv[part, 0]
+        for k in range(1, cam_count):
+            summed = summed + partial_recv[part, k]
+        total[part, 0] = summed
+        for k in near_first[::-1]:
+            to_cam_own(TOTAL + part, total.at[part, 0], total.at[part], k).start()
+
+    def give_back(places, part):
+        def awaited(k):
+            @pl.when(k != 0)
+            def _():
+                from_cam(TOTAL + part, total.at[part], k).wait_recv()
+
+        for k in places:
+            awaited(k)
+
+        def one(i, carry):
+            here = pl.ds(pl.multiple_of(i * piece_tile, piece_tile), piece_tile)
+            at = pl.ds(pl.multiple_of(part * part_count + i * piece_tile, piece_tile), piece_tile)
+            summed = returned[...]
+            for k in places:
+                scaled = grad_rows[part, k, :, here] * total[part, k, :, here]
+                w = weight[k, :, at]
+                products = jnp.concatenate([w * scaled[f:f + 1] for f in range(per_group)], axis=0)
+                high, low = split(products)
+                both = jnp.concatenate([high, low], axis=0)
+                summed = summed + dot(both, one_hot[k, :, at], ((1,), (1,)))
+            returned[...] = summed
+            return carry
+        lax.fori_loop(0, part_count // piece_tile, one, 0)
+
+    def listed(i, places):
+        k = jnp.int32(places[0])
+        for at, which in enumerate(places):
+            k = jnp.where(i == at, which, k)
+        return k
+
+    out_order = near_first[::-1] + [0]
+    back_order = [0] + near_first
+
+    def project_some(start, stop, part):
+        def one(i, carry):
+            project([listed(i, out_order[0::2]), listed(i, out_order[1::2])], part)
+            return carry
+        lax.fori_loop(start, stop, one, 0)
+
+    def give_back_some(start, stop, part):
+        def one(i, carry):
+            give_back([listed(i, back_order[0::2]), listed(i, back_order[1::2])], part)
+            return carry
+        lax.fori_loop(start, stop, one, 0)
+
+    pairs_count = cam_count // 2
+    late_sum = 1
+    project_some(0, pairs_count, 0)
+    build_far(1)
+    project_some(0, pairs_count, 1)
+    sum_up(0)
+    returned[...] = jnp.zeros_like(returned)
     to_frame(0).wait_recv()
     to_frame(1).wait_recv()
     ids = lax.broadcasted_iota(jnp.int32, (width, width), 0)
@@ -332,115 +465,6 @@
     rest_recv[0] = rest_send[group]
 
 
-    def build_far(i, carry):
-        k = place(i)
-        from_cam(PIXELS, pixels, k).wait_recv()
-        build(k)
-        return carry
-
-    lax.fori_loop(near_count + 1, cam_count, build_far, 0)
-
-    from_nodes(VISIBLE, visible_recv).wait_recv()
-    unpack(square, visible_recv)
-    high, low = split(jnp.transpose(square[...])[0:rows, 0:keys])
-    table[0:rows] = high
-    table[rows:2 * rows] = low
-
-    piece_tile = tiles[1]
-    part_count = pixel_count // PARTS
-
-    def project(places, part):
-        def awaited(k):
-            @pl.when(jnp.logical_and(k != 0, jnp.where(half == 0, k <= opposite, k >= opposite)))
-            def _():
-                from_cam(GRADS, grad_rows, k).wait_recv()
-
-        def send(k):
-            @pl.when(k != 0)
-            def _():
-                to_cam(PARTIAL + part, partial.at[part, k], partial_recv.at[part], k).start()
-
-        if part == 0:
-            for k in places:
-                awaited(k)
-
-        def one(i, carry):
-            here = pl.ds(pl.multiple_of(i * piece_tile, piece_tile), piece_tile)
-            at = pl.ds(pl.multiple_of(part * part_count + i * piece_tile, piece_tile), piece_tile)
-            for k in places:
-                picked = dot(table[...], one_hot[k, :, at], ((1,), (0,)))
-                g = grad_rows[k, :, at]
-                summed = jnp.zeros((span, piece_tile), jnp.float32)
-                for f in range(per_group):
-                    piece = picked[f * span:(f + 1) * span] + picked[rows + f * span:rows + (f + 1) * span]
-                    summed = summed + piece * g[f:f + 1]
-                partial[part, k, :, here] = jnp.sum(summed * weight[k, :, at], axis=0, keepdims=True)
-            return carry
-        lax.fori_loop(0, part_count // piece_tile, one, 0)
-        for k in places:
-            send(k)
-
-    def sum_up(part):
-        partial_recv[part, 0] = partial[part, 0]
-        from_cams(PARTIAL + part, partial_recv.at[part]).wait_recv()
-        summed = partial_recv[part, 0]
-        for k in range(1, cam_count):
-            summed = summed + partial_recv[part, k]
-        total[part, 0] = summed
-        for k in near_first[::-1]:
-            to_cam_own(TOTAL + part, total.at[part, 0], total.at[part], k).start()
-
-    def give_back(places, part):
-        def awaited(k):
-            @pl.when(k != 0)
-            def _():
-                from_cam(TOTAL + part, total.at[part], k).wait_recv()
-
-        for k in places:
-            awaited(k)
-
-        def one(i, carry):
-            here = pl.ds(pl.multiple_of(i * piece_tile, piece_tile), piece_tile)
-            at = pl.ds(pl.multiple_of(part * part_count + i * piece_tile, piece_tile), piece_tile)
-            summed = returned[...]
-            for k in places:
-                scaled = grad_rows[k, :, at] * total[part, k, :, here]
-                w = weight[k, :, at]
-                products = jnp.concatenate([w * scaled[f:f + 1] for f in range(per_group)], axis=0)
-                high, low = split(products)
-                both = jnp.concatenate([high, low], axis=0)
-                summed = summed + dot(both, one_hot[k, :, at], ((1,), (1,)))
-            returned[...] = summed
-            return carry
-        lax.fori_loop(0, part_count // piece_tile, one, 0)
-
-    def listed(i, places):
-        k = jnp.int32(places[0])
-        for at, which in enumerate(places):
-            k = jnp.where(i == at, which, k)
-        return k
-
-    out_order = near_first[::-1] + [0]
-    back_order = [0] + near_first
-
-    def project_some(start, stop, part):
-        def one(i, carry):
-            project([listed(i, out_order[0::2]), listed(i, out_order[1::2])], part)
-            return carry
-        lax.fori_loop(start, stop, one, 0)
-
-    def give_back_some(start, stop, part):
-        def one(i, carry):
-            give_back([listed(i, back_order[0::2]), listed(i, back_order[1::2])], part)
-            return carry
-        lax.fori_loop(start, stop, one, 0)
-
-    pairs_count = cam_count // 2
-    late_sum = 1
-    project_some(0, pairs_count, 0)
-    project_some(0, pairs_count, 1)
-    sum_up(0)
-    returned[...] = jnp.zeros_like(returned)
     each_cam(lambda k: to_cam(REST, rest_send.at[peer_group(k)], rest_recv, k).start())
     give_back_some(0, late_sum, 0)
     sum_up(1)
@@ -519,11 +543,13 @@
         result[2 * params + f] = precond[f] * left + ratio * direction[f]
 
     for phase, target in (
-        (PIXELS, pixels), (GRADS, grad_rows), (OWNED, owned_recv), (REST, rest_recv),
+        (OWNED, owned_recv), (REST, rest_recv),
         (IMAGE, image_recv), (SUMS, cam_sums),
     ):
         from_cams(phase, target).wait_send()
     for part in range(PARTS):
+        from_cams(PIXELS + part, pixels.at[part]).wait_send()
+        from_cams(GRADS + part, grad_rows.at[part]).wait_send()
         from_cams(TOTAL + part, total.at[part]).wait_send()
         from_cams(PARTIAL + part, partial_recv.at[part]).wait_send()
     to_frame(0).wait_send()
@@ -546,7 +572,7 @@
         held = local * cam_count
         keys = slots * node_count
         part_count = pixel_count // PARTS
-        tiles = (min(TILES[0], pixel_count), min(TILES[1], part_count))
+        tiles = tuple(min(size, part_count) for size in TILES)
         up = lambda size, to: (size + to - 1) // to * to
         side = up(max(rows, keys), 128)
         message = slots * (per_group // 2) + (per_group % 2) * ((slots + 1) // 2)
@@ -566,9 +592,9 @@
             out_specs=vmem,
             scratch_shapes=[
                 *(pltpu.VMEM(value.shape, value.dtype) for value in inputs),
-                pltpu.VMEM((cam_count, 8, pixel_count), f32),
-                pltpu.VMEM((groups, per_group, pixel_count), f32),
-                pltpu.VMEM((cam_count, per_group, pixel_count), f32),
+                pltpu.VMEM((PARTS, cam_count, 8, part_count), f32),
+                pltpu.VMEM((PARTS, groups, per_group, part_count), f32),
+                pltpu.VMEM((PARTS, cam_count, per_group, part_count), f32),
                 pltpu.VMEM((cam_count, keys, pixel_count), bf16),
                 pltpu.VMEM((cam_count, span, pixel_count), f32),
                 pltpu.VMEM(slice_shape, f32),
@@ -596,9 +622,9 @@
                 pltpu.VMEM((node_count, 1, width), f32),
                 pltpu.VMEM((cam_count, 1, width), f32),
                 pltpu.VMEM((1, 1, width), f32),
-                dma((10,)),
-                dma((10,)),
-                dma((4, cam_count)),
+                dma((12,)),
+                dma((12,)),
+                dma((6, cam_count)),
                 dma((3,)),
                 dma((3,)),
                 dma((2,)),

time: 66.5 us -> 64.8 us (0.974)
  Pallas kernels: 64.3 us -> 62.6 us
    pallas_call x1, Pallas kernels: 64.3 us -> 62.6 us  [on_device(): pl.pallas_call(functools.partial(kernel, node_count, cam_count, tiles), o...]
where the time goes in v5:
time: 64.8 us; the launch traced here: 64.6 us
  Pallas kernels  62.6 us (97%)
  local copies, waits for them, and re-layouts  1.35 us (2%)
    pallas_call x1, Pallas kernels, on_device(): pl.pallas_call(functools.partial(kernel, node_count, cam_count, tiles), o...  62.6 us
    transpose x1, local copies, waits for them, and re-layouts, on_device(): turn = lambda value: jnp.transpose(value, (1, 0, 2))  1.35 us

profile of v5, /device:TPU:1, one launch (start us, length us, event | category | flops | bytes accessed | tf_op | source)
XLA Modules:
  0.0 64.6 jit_solution(10294802280217722017)
XLA Ops:
  0.6 62.6 %cg_step.1 = f32[36,2,128]{2,1,0:T(2,128)} custom-call(f32[12,2,128]{2,1,0:T(2,128)} %bitcast.12, f32[12,2,128]{2,1,0:T(2,128)} %bitcast.13, f32[12,2,128]{2,1,0:T(2,128)} %bitcast.14, f32[12,2,128]{2,1,0:T(2,128)} %bitcast.15, s32[3,1,64]{2,1,0:T(1,128)} %bitcast.17, bf16[12,2048]{1,0:T(8,128)(2,1)} %grads_in.1, s32[4,2048]{1,0:T(4,128)} %node_refs_in.1, ...), custom_call_target="tpu_custom_call" | custom-call | tf_op jit(solution)/shard_map/cg_step/pallas_call | solution.py:588
  63.3 1.4 %slice_bitcast_fusion = (f32[2,12,128]{2,0,1:T(2,128)}, f32[2,12,128]{2,0,1:T(2,128)}, f32[2,12,128]{2,0,1:T(2,128)}) fusion(f32[36,2,128]{2,1,0:T(2,128)} %cg_step.1), kind=kLoop, calls=%fused_computation | loop fusion | bytes 73728 | tf_op jit(solution)/shard_map/transpose | solution.py:579

commit v6 on v5

--- a/solution.py
+++ b/solution.py
@@ -12,6 +12,7 @@
 REACH = 2
 TILES = (512, 1024)
 PARTS = 2
+QUAD = 4
 HALVES = 2
 temporal_weight = 0.5
 rigid_weight = 0.1
@@ -425,7 +426,7 @@
 
     def project_some(start, stop, part):
         def one(i, carry):
-            project([listed(i, out_order[0::2]), listed(i, out_order[1::2])], part)
+            project([listed(i, out_order[at::QUAD]) for at in range(QUAD)], part)
             return carry
         lax.fori_loop(start, stop, one, 0)
 
@@ -436,10 +437,9 @@
         lax.fori_loop(start, stop, one, 0)
 
     pairs_count = cam_count // 2
-    late_sum = 1
-    project_some(0, pairs_count, 0)
+    project_some(0, cam_count // QUAD, 0)
     build_far(1)
-    project_some(0, pairs_count, 1)
+    project_some(0, cam_count // QUAD, 1)
     sum_up(0)
     returned[...] = jnp.zeros_like(returned)
     to_frame(0).wait_recv()
@@ -466,9 +466,8 @@
 
 
     each_cam(lambda k: to_cam(REST, rest_send.at[peer_group(k)], rest_recv, k).start())
-    give_back_some(0, late_sum, 0)
     sum_up(1)
-    give_back_some(late_sum, pairs_count, 0)
+    give_back_some(0, pairs_count, 0)
     give_back_some(0, pairs_count, 1)
     square[...] = jnp.zeros_like(square)
     square[0:rows, 0:keys] = returned[0:rows] + returned[rows:2 * rows]

time: 64.8 us -> 63.7 us (0.983)
  Pallas kernels: 62.6 us -> 61.5 us
    pallas_call x1, Pallas kernels: 62.6 us -> 61.5 us  [on_device(): pl.pallas_call(functools.partial(kernel, node_count, cam_count, tiles), o...]
where the time goes in v6:
time: 63.7 us; the launch traced here: 63.5 us
  Pallas kernels  61.5 us (97%)
  local copies, waits for them, and re-layouts  1.35 us (2%)
  between operations  0.64 us (1%)
    pallas_call x1, Pallas kernels, on_device(): pl.pallas_call(functools.partial(kernel, node_count, cam_count, tiles), o...  61.5 us
    transpose x1, local copies, waits for them, and re-layouts, on_device(): turn = lambda value: jnp.transpose(value, (1, 0, 2))  1.35 us

profile of v6, /device:TPU:1, one launch (start us, length us, event | category | flops | bytes accessed | tf_op | source)
XLA Modules:
  0.0 63.5 jit_solution(14255009232780702618)
XLA Ops:
  0.6 61.5 %cg_step.1 = f32[36,2,128]{2,1,0:T(2,128)} custom-call(f32[12,2,128]{2,1,0:T(2,128)} %bitcast.12, f32[12,2,128]{2,1,0:T(2,128)} %bitcast.13, f32[12,2,128]{2,1,0:T(2,128)} %bitcast.14, f32[12,2,128]{2,1,0:T(2,128)} %bitcast.15, s32[3,1,64]{2,1,0:T(1,128)} %bitcast.17, bf16[12,2048]{1,0:T(8,128)(2,1)} %grads_in.1, s32[4,2048]{1,0:T(4,128)} %node_refs_in.1, ...), custom_call_target="tpu_custom_call" | custom-call | tf_op jit(solution)/shard_map/cg_step/pallas_call | solution.py:587
  62.1 1.4 %slice_bitcast_fusion = (f32[2,12,128]{2,0,1:T(2,128)}, f32[2,12,128]{2,0,1:T(2,128)}, f32[2,12,128]{2,0,1:T(2,128)}) fusion(f32[36,2,128]{2,1,0:T(2,128)} %cg_step.1), kind=kLoop, calls=%fused_computation | loop fusion | bytes 73728 | tf_op jit(solution)/shard_map/transpose | solution.py:578

commit v7 on v6

--- a/solution.py
+++ b/solution.py
@@ -432,11 +432,10 @@
 
     def give_back_some(start, stop, part):
         def one(i, carry):
-            give_back([listed(i, back_order[0::2]), listed(i, back_order[1::2])], part)
+            give_back([listed(i, back_order[at::QUAD]) for at in range(QUAD)], part)
             return carry
         lax.fori_loop(start, stop, one, 0)
 
-    pairs_count = cam_count // 2
     project_some(0, cam_count // QUAD, 0)
     build_far(1)
     project_some(0, cam_count // QUAD, 1)
@@ -467,8 +466,8 @@
 
     each_cam(lambda k: to_cam(REST, rest_send.at[peer_group(k)], rest_recv, k).start())
     sum_up(1)
-    give_back_some(0, pairs_count, 0)
-    give_back_some(0, pairs_count, 1)
+    give_back_some(0, cam_count // QUAD, 0)
+    give_back_some(0, cam_count // QUAD, 1)
     square[...] = jnp.zeros_like(square)
     square[0:rows, 0:keys] = returned[0:rows] + returned[rows:2 * rows]
     by_key = jnp.transpose(square[...])

time: 63.7 us -> 64.1 us (level)
  no operation moved by 1% of the time
where the time goes in v7:
time: 64.1 us; the launch traced here: 63.9 us
  Pallas kernels  61.9 us (97%)
  local copies, waits for them, and re-layouts  1.35 us (2%)
    pallas_call x1, Pallas kernels, on_device(): pl.pallas_call(functools.partial(kernel, node_count, cam_count, tiles), o...  61.9 us
    transpose x1, local copies, waits for them, and re-layouts, on_device(): turn = lambda value: jnp.transpose(value, (1, 0, 2))  1.35 us

profile of v7, /device:TPU:1, one launch (start us, length us, event | category | flops | bytes accessed | tf_op | source)
XLA Modules:
  0.0 63.9 jit_solution(6175943341311698180)
XLA Ops:
  0.6 61.9 %cg_step.1 = f32[36,2,128]{2,1,0:T(2,128)} custom-call(f32[12,2,128]{2,1,0:T(2,128)} %bitcast.12, f32[12,2,128]{2,1,0:T(2,128)} %bitcast.13, f32[12,2,128]{2,1,0:T(2,128)} %bitcast.14, f32[12,2,128]{2,1,0:T(2,128)} %bitcast.15, s32[3,1,64]{2,1,0:T(1,128)} %bitcast.17, bf16[12,2048]{1,0:T(8,128)(2,1)} %grads_in.1, s32[4,2048]{1,0:T(4,128)} %node_refs_in.1, ...), custom_call_target="tpu_custom_call" | custom-call | tf_op jit(solution)/shard_map/cg_step/pallas_call | solution.py:586
  62.5 1.4 %slice_bitcast_fusion = (f32[2,12,128]{2,0,1:T(2,128)}, f32[2,12,128]{2,0,1:T(2,128)}, f32[2,12,128]{2,0,1:T(2,128)}) fusion(f32[36,2,128]{2,1,0:T(2,128)} %cg_step.1), kind=kLoop, calls=%fused_computation | loop fusion | bytes 73728 | tf_op jit(solution)/shard_map/transpose | solution.py:577
